TPU v7x, 256 devices: a whole 4x4x8 slice. The times are simulated.
256 devices in a mesh: px: 32 (over z_lo, y, x), py: 8 (over z_hi, core).
Axes of the slice: x: 4, y: 4, z: 8 (z_hi: 4, z_lo: 2; z = z_hi * 2 + z_lo), core: 2. Of those that a mesh axis runs over, the one named last changes fastest.
Arguments:
- log_source: float32 [256, 256, 256], P('px', 'py'), may hold values from -12 to 240, as said below
- log_target: float32 [256, 256, 256], P('px', 'py'), may hold values from -12 to 240, as said below
Outputs:
- potential_f: float32 [256, 256, 256], P('px', 'py')
- potential_g: float32 [256, 256, 256], P('px', 'py')
Inputs may be any that keep to these rules, and one draw needn't show every extreme that they name: `log_source`: Log-density values on every cell. `log_target`: Log-density values on every cell.
All inputs are finite; a program needn't handle non-finite values.
Results may differ from a plain program's by a relative error of at most 0.0001.
Values sent between devices are 32-bit elements; how exact they have to be, the bound alone decides.
A program may use at most 128 MiB of HBM per device.

v0:
```python
from functools import partial
import math

import jax
import jax.numpy as jnp
from jax import lax
from jax.sharding import PartitionSpec as P

LEVELS = 3
ITERS = 2
FINE_ITERS = 1
BAND = 16


def epsilon_of(level_index):
    return 0.05 * 2.0 ** (LEVELS - 1 - level_index)


def soft_axis(values, along, level_index):
    inverse_width = 2.0 ** (LEVELS - 1 - level_index) / 18.0
    window = [1, 1, 1]
    window[along] = 2 * BAND + 1
    padding = [(0, 0), (0, 0), (0, 0)]
    padding[along] = (BAND, BAND)
    line_max = lax.reduce_window(
        values, -jnp.inf, lax.max, tuple(window), (1, 1, 1), tuple(padding)
    )
    padded = jnp.pad(values, padding, constant_values=-jnp.inf)
    length = values.shape[along]
    summed = jnp.zeros_like(values)
    for offset in range(2 * BAND + 1):
        shifted = lax.slice_in_dim(padded, offset, offset + length, axis=along)
        weight = math.exp(-float((offset - BAND) ** 2) * inverse_width)
        summed = summed + weight * jnp.exp(shifted - line_max)
    return line_max + jnp.log(summed)


def restrict(values):
    size_a, size_b, size_c = values.shape
    blocks = values.reshape(size_a // 2, 2, size_b // 2, 2, size_c // 2, 2)
    block_max = jnp.max(blocks, axis=(1, 3, 5), keepdims=True)
    merged = block_max + jnp.log(
        jnp.mean(jnp.exp(blocks - block_max), axis=(1, 3, 5), keepdims=True)
    )
    return merged.reshape(size_a // 2, size_b // 2, size_c // 2)


def prolong(values):
    return jnp.repeat(jnp.repeat(jnp.repeat(values, 2, axis=0), 2, axis=1), 2, axis=2)


def unchanged(values):
    return values


def forward(values, rows_fn, columns_fn):
    middle = rows_fn(lax.all_to_all(values, "py", split_axis=2, concat_axis=1, tiled=True))
    return columns_fn(lax.all_to_all(middle, "px", split_axis=1, concat_axis=0, tiled=True))


def backward(values, rows_fn, depth_fn):
    middle = rows_fn(lax.all_to_all(values, "px", split_axis=0, concat_axis=1, tiled=True))
    return depth_fn(lax.all_to_all(middle, "py", split_axis=1, concat_axis=2, tiled=True))


def pencil_level(level_index, source_level, target_level, potential_g):
    epsilon = epsilon_of(level_index)
    sweeps = FINE_ITERS if level_index == LEVELS - 1 else ITERS
    along_first = partial(soft_axis, along=0, level_index=level_index)
    along_second = partial(soft_axis, along=1, level_index=level_index)
    along_third = partial(soft_axis, along=2, level_index=level_index)
    potential_f = potential_g
    source_turned = forward(source_level, unchanged, unchanged)
    turned_f = source_turned
    for iteration in range(sweeps):
        reached = forward(along_third(potential_g / epsilon), along_second, along_first)
        turned_f = epsilon * (source_turned - reached)
        pulled = backward(along_first(turned_f / epsilon), along_second, along_third)
        potential_g = epsilon * (target_level - pulled)
    if level_index == LEVELS - 1:
        potential_f = backward(turned_f, unchanged, unchanged)
    return (potential_f, potential_g)


def per_device(log_source, log_target):
    sources = [log_source]
    targets = [log_target]
    for level_index in range(LEVELS - 1):
        sources = sources + [restrict(sources[-1])]
        targets = targets + [restrict(targets[-1])]
    sources = sources[::-1]
    targets = targets[::-1]
    potential_g = jnp.zeros_like(sources[0])
    potential_f = potential_g
    first_level = 0
    for level_index in range(first_level, LEVELS):
        potential_f, potential_g = pencil_level(
            level_index, sources[level_index], targets[level_index], potential_g
        )
        if level_index < LEVELS - 1:
            potential_g = prolong(potential_g)
    return (potential_f, potential_g)


def solution(mesh):
    return jax.shard_map(
        per_device,
        mesh=mesh,
        in_specs=(P("px", "py", None), P("px", "py", None)),
        out_specs=(P("px", "py", None), P("px", "py", None)),
        check_vma=False,
    )
```

profile of v0, /device:TPU:1, one launch (start us, length us, event | category | flops | bytes accessed | tf_op | source)
XLA Modules:
  0.0 639.6 jit_solution(10024164577190180262)
XLA Ops:
  0.6 18.9 %reshape.69 = f32[4,2,16,2,128,2]{5,4,3,2,1,0:T(8,128)} reshape(f32[8,32,256]{2,1,0:T(8,128)} %param.2) | data formatting | bytes 524288 | tf_op jit(solution)/shard_map/reshape | solution.py:40
  19.5 7.0 %reduce_max.37 = f32[4,16,128]{2,1,0:T(8,128)S(1)} reduce(f32[4,2,16,2,128,2]{5,4,3,2,1,0:T(8,128)} %reshape.69, f32[]{:T(128)} %constant.46.clone.1), dimensions={1,3,5}, to_apply=%region_2.0 | reduce | flops 57344 | bytes 294916 | tf_op jit(solution)/shard_map/reduce_max | solution.py:41
  26.5 8.2 %exponential_reduce_fusion = f32[4,16,128]{2,1,0:T(8,128)S(1)} fusion(f32[4,2,16,2,128,2]{5,4,3,2,1,0:T(8,128)} %reshape.69, f32[4,16,128]{2,1,0:T(8,128)S(1)} %reduce_max.37), kind=kLoop, calls=%fused_computation | loop fusion | flops 122880 | bytes 327680 | tf_op jit(solution)/shard_map/reduce_sum | solution.py:43
  38.5 10.0 %all-to-all-start.4 = ((f32[8,1,128]{2,1,0:T(1,128)}), f32[8,1,128]{2,1,0:T(1,128)S(1)}, u32[]{:S(2)}, u32[]{:S(2)}) async-start(f32[8,1,128]{2,1,0:T(1,128)} %reshape.78), calls=%async_computation.4 | async-start | bytes 8192 | tf_op jit(solution)/shard_map/all_to_all | solution.py:57
  59.3 18.1 %reshape.68 = f32[4,2,16,2,128,2]{5,4,3,2,1,0:T(8,128)} reshape(f32[8,32,256]{2,1,0:T(8,128)S(1)} %copy-done.1) | data formatting | bytes 524288 | tf_op jit(solution)/shard_map/reshape | solution.py:40
  86.4 7.5 %all-to-all-start.5 = ((f32[2,64,8]{2,0,1:T(2,128)}), f32[2,64,8]{2,0,1:T(2,128)S(1)}, u32[]{:S(2)}, u32[]{:S(2)}) async-start(f32[2,64,8]{2,0,1:T(2,128)} %bitcast.15), calls=%async_computation.5 | async-start | bytes 131072 | tf_op jit(solution)/shard_map/all_to_all | solution.py:58
  105.4 8.2 %exponential_reduce_fusion.1 = f32[4,16,128]{2,1,0:T(8,128)S(1)} fusion(f32[4,2,16,2,128,2]{5,4,3,2,1,0:T(8,128)} %reshape.68, f32[4,16,128]{2,1,0:T(8,128)S(1)} %reduce_max.36), kind=kLoop, calls=%fused_computation.1 | loop fusion | flops 122880 | bytes 327680 | tf_op jit(solution)/shard_map/reduce_sum | solution.py:43
  121.6 7.9 %all-to-all-start.8 = ((f32[64,2,8]{2,1,0:T(2,128)}), f32[64,2,8]{2,1,0:T(2,128)S(1)}, u32[]{:S(2)}, u32[]{:S(2)}) async-start(f32[64,2,8]{2,1,0:T(2,128)} %log_add_fusion.10), calls=%async_computation.8 | async-start | bytes 131072 | tf_op jit(solution)/shard_map/all_to_all | solution.py:62
  138.4 10.1 %all-to-all-start.9 = ((f32[8,1,128]{2,1,0:T(1,128)}), f32[8,1,128]{2,1,0:T(1,128)S(1)}, u32[]{:S(2)}, u32[]{:S(2)}) async-start(f32[8,1,128]{2,1,0:T(1,128)} %reshape.82), calls=%async_computation.9 | async-start | bytes 8192 | tf_op jit(solution)/shard_map/all_to_all | solution.py:63
  158.2 10.1 %all_to_all.504 = f32[8,1,128]{2,1,0:T(1,128)S(1)} all-to-all(f32[8,1,128]{2,1,0:T(1,128)S(1)} %reshape.84), channel_id=1, replica_groups=mesh['px'=32,'py'=8] {'py'}, dimensions={0} | all-to-all | bytes 8192 | tf_op jit(solution)/shard_map/all_to_all | solution.py:57
  170.1 10.8 %all_to_all.505 = f32[2,64,8]{2,0,1:T(2,128)S(1)} all-to-all(f32[2,64,8]{2,0,1:T(2,128)S(1)} %copy.127), channel_id=1, replica_groups=mesh['px'=32,'py'=8] {'px'}, dimensions={1} | all-to-all | bytes 8192 | tf_op jit(solution)/shard_map/all_to_all | solution.py:58
  188.2 10.6 %all_to_all.506 = f32[64,2,8]{2,1,0:T(2,128)S(1)} all-to-all(f32[64,2,8]{2,1,0:T(2,128)S(1)} %log_add_fusion.7), channel_id=1, replica_groups=mesh['px'=32,'py'=8] {'px'}, dimensions={0} | all-to-all | bytes 8192 | tf_op jit(solution)/shard_map/all_to_all | solution.py:62
  277.8 10.7 %all_to_all.507 = f32[32,1,256]{2,1,0:T(1,128)S(1)} all-to-all(f32[32,1,256]{2,1,0:T(1,128)S(1)} %reshape.92), channel_id=1, replica_groups=mesh['px'=32,'py'=8] {'px'}, dimensions={0} | all-to-all | bytes 65536 | tf_op jit(solution)/shard_map/all_to_all | solution.py:62
  293.7 13.1 %all_to_all.508 = f32[8,1,1024]{2,1,0:T(1,128)S(1)} all-to-all(f32[8,1,1024]{2,1,0:T(1,128)S(1)} %reshape.94), channel_id=1, replica_groups=mesh['px'=32,'py'=8] {'py'}, dimensions={0} | all-to-all | bytes 65536 | tf_op jit(solution)/shard_map/all_to_all | solution.py:63
  314.1 10.2 %all_to_all.509 = f32[8,1,1024]{2,1,0:T(1,128)S(1)} all-to-all(f32[8,1,1024]{2,1,0:T(1,128)S(1)} %reshape.96), channel_id=1, replica_groups=mesh['px'=32,'py'=8] {'py'}, dimensions={0} | all-to-all | bytes 65536 | tf_op jit(solution)/shard_map/all_to_all | solution.py:57
  329.7 11.0 %all_to_all.510 = f32[32,1,256]{2,1,0:T(1,128)S(1)} all-to-all(f32[32,1,256]{2,1,0:T(1,128)S(1)} %reshape.98), channel_id=1, replica_groups=mesh['px'=32,'py'=8] {'px'}, dimensions={0} | all-to-all | bytes 65536 | tf_op jit(solution)/shard_map/all_to_all | solution.py:58
  355.3 10.5 %all_to_all.511 = f32[32,1,256]{2,1,0:T(1,128)S(1)} all-to-all(f32[32,1,256]{2,1,0:T(1,128)S(1)} %reshape.100), channel_id=1, replica_groups=mesh['px'=32,'py'=8] {'px'}, dimensions={0} | all-to-all | bytes 65536 | tf_op jit(solution)/shard_map/all_to_all | solution.py:62
  394.5 9.6 %reduce_window_max.288 = f32[8,32,256]{2,1,0:T(8,128)S(1)} reduce-window(f32[8,32,256]{2,1,0:T(8,128)S(1)} %copy.152, f32[]{:T(128)} %constant.46.clone.1), window={size=1x1x33 pad=0_0x0_0x16_16}, to_apply=%region_31.32 | reduce-window | flops 2097152 | bytes 524292 | tf_op jit(solution)/shard_map/reduce_window_max | solution.py:25
  408.1 7.2 %all-to-all-start.22 = ((f32[8,1,8192]{2,1,0:T(1,128)}), f32[8,1,8192]{2,1,0:T(1,128)S(1)}, u32[]{:S(2)}, u32[]{:S(2)}) async-start(f32[8,1,8192]{2,1,0:T(1,128)} %reshape.104), calls=%async_computation.22 | async-start | bytes 524288 | tf_op jit(solution)/shard_map/all_to_all | solution.py:57
  431.3 18.9 %fusion.2788 = f32[8,256,32]{2,0,1:T(8,128)S(1)} fusion(f32[8,256,32]{2,0,1:T(8,128)S(1)} %bitcast.225), kind=kOutput, calls=%fused_computation.3558 | output fusion | flops 2097152 | bytes 524288 | tf_op jit(solution)/shard_map/reduce_window_max | solution.py:25
  450.1 11.8 %fusion.2778 = f32[256,8,32]{2,1,0:T(8,128)S(1)} fusion(f32[8,256,32]{2,0,1:T(8,128)S(1)} %fusion.2788, f32[8,256,32]{2,0,1:T(8,128)S(1)} %bitcast.226), kind=kLoop, calls=%fused_computation.3541 | loop fusion | flops 6422528 | bytes 786432
  463.1 7.8 %all-to-all-start.23 = ((f32[32,1,2048]{2,1,0:T(1,128)}), f32[32,1,2048]{2,1,0:T(1,128)S(1)}, u32[]{:S(2)}, u32[]{:S(2)}) async-start(f32[32,1,2048]{2,1,0:T(1,128)} %reshape.106), calls=%async_computation.23 | async-start | bytes 524288 | tf_op jit(solution)/shard_map/all_to_all | solution.py:58
  480.5 18.9 %fusion.2789 = f32[256,8,32]{2,1,0:T(8,128)S(1)} fusion(f32[256,8,32]{2,1,0:T(8,128)S(1)} %bitcast.209), kind=kOutput, calls=%fused_computation.3559 | output fusion | flops 2097152 | bytes 524288 | tf_op jit(solution)/shard_map/reduce_window_max | solution.py:25
  499.4 11.9 %broadcast_multiply_fusion = (f32[256,8,32]{2,1,0:T(8,128)S(1)}, f32[256,8,32]{2,1,0:T(8,128)S(1)}) fusion(f32[256,8,32]{2,1,0:T(8,128)S(1)} %fusion.2789, f32[256,8,32]{2,1,0:T(8,128)S(1)} %bitcast.210, f32[32,8,8,32]{3,2,1,0:T(8,128)S(1)} %copy.107), kind=kLoop, calls=%fused_computation.802 | loop fusion | flops 6553600 | bytes 1310720 | tf_op jit(solution)/shard_map/mul | solution.py:77
  516.4 18.9 %fusion.2790 = f32[256,8,32]{2,1,0:T(8,128)S(1)} fusion(f32[256,8,32]{2,1,0:T(8,128)S(1)} %get-tuple-element.3), kind=kOutput, calls=%fused_computation.3560 | output fusion | flops 2097152 | bytes 524288 | tf_op jit(solution)/shard_map/reduce_window_max | solution.py:25
  535.2 11.8 %log_add_fusion.1 = f32[256,8,32]{2,1,0:T(8,128)S(1)} fusion(f32[256,8,32]{2,1,0:T(8,128)S(1)} %fusion.2790, f32[256,8,32]{2,1,0:T(8,128)S(1)} %get-tuple-element.3), kind=kLoop, calls=%fused_computation.222 | loop fusion | flops 6422528 | bytes 786432 | tf_op jit(solution)/shard_map/add | solution.py:35
  548.2 7.8 %all-to-all-start.26 = ((f32[32,1,2048]{2,1,0:T(1,128)}), f32[32,1,2048]{2,1,0:T(1,128)S(1)}, u32[]{:S(2)}, u32[]{:S(2)}) async-start(f32[32,1,2048]{2,1,0:T(1,128)} %reshape.112), calls=%async_computation.26 | async-start | bytes 524288 | tf_op jit(solution)/shard_map/all_to_all | solution.py:62
  563.8 9.3 %all-to-all-start.25 = ((f32[8,1,8192]{2,1,0:T(1,128)}), f32[8,1,8192]{2,1,0:T(1,128)S(1)}, u32[]{:S(2)}, u32[]{:S(2)}) async-start(f32[8,1,8192]{2,1,0:T(1,128)} %reshape.110), calls=%async_computation.25 | async-start | bytes 524288 | tf_op jit(solution)/shard_map/all_to_all | solution.py:63
  574.9 18.9 %fusion.2791 = f32[8,256,32]{2,0,1:T(8,128)S(1)} fusion(f32[8,256,32]{2,0,1:T(8,128)S(1)} %bitcast.227), kind=kOutput, calls=%fused_computation.3561 | output fusion | flops 2097152 | bytes 524288 | tf_op jit(solution)/shard_map/reduce_window_max | solution.py:25
  593.8 11.8 %fusion.2779 = f32[256,8,32]{2,1,0:T(8,128)S(1)} fusion(f32[8,256,32]{2,0,1:T(8,128)S(1)} %fusion.2791, f32[8,256,32]{2,0,1:T(8,128)S(1)} %bitcast.228), kind=kLoop, calls=%fused_computation.3542 | loop fusion | flops 6422528 | bytes 786432
  606.7 7.2 %all-to-all-start.27 = ((f32[8,1,8192]{2,1,0:T(1,128)}), f32[8,1,8192]{2,1,0:T(1,128)S(1)}, u32[]{:S(2)}, u32[]{:S(2)}) async-start(f32[8,1,8192]{2,1,0:T(1,128)} %reshape.114), calls=%async_computation.27 | async-start | bytes 524288 | tf_op jit(solution)/shard_map/all_to_all | solution.py:63
  626.5 9.6 %reduce_window_max.293 = f32[8,32,256]{2,1,0:T(8,128)S(1)} reduce-window(f32[8,32,256]{2,1,0:T(8,128)S(1)} %all_to_all.475, f32[]{:T(128)} %constant.46.clone.1), window={size=1x1x33 pad=0_0x0_0x16_16}, to_apply=%region_36.37 | reduce-window | flops 2097152 | bytes 524292 | tf_op jit(solution)/shard_map/reduce_window_max | solution.py:25
  (231 shorter events, 273.1 us)
Async XLA Ops:
  36.8 22.5 %copy-start.1 = (f32[8,32,256]{2,1,0:T(8,128)S(1)}, f32[8,32,256]{2,1,0:T(8,128)}, u32[]{:S(2)}) copy-start(f32[8,32,256]{2,1,0:T(8,128)} %param.3) | copy-start | bytes 786436
  38.5 16.9 %all-to-all-start.4 = ((f32[8,1,128]{2,1,0:T(1,128)}), f32[8,1,128]{2,1,0:T(1,128)S(1)}, u32[]{:S(2)}, u32[]{:S(2)}) async-start(f32[8,1,128]{2,1,0:T(1,128)} %reshape.78), calls=%async_computation.4 | async-start | bytes 8192 | tf_op jit(solution)/shard_map/all_to_all | solution.py:57
  55.4 31.0 %all-to-all-start.6 = ((f32[8,1,128]{2,1,0:T(1,128)}), f32[8,1,128]{2,1,0:T(1,128)S(1)}, u32[]{:S(2)}, u32[]{:S(2)}) async-start(f32[8,1,128]{2,1,0:T(1,128)} %reshape.80), calls=%async_computation.6 | async-start | bytes 8192 | tf_op jit(solution)/shard_map/all_to_all | solution.py:57
  86.4 14.9 %all-to-all-start.5 = ((f32[2,64,8]{2,0,1:T(2,128)}), f32[2,64,8]{2,0,1:T(2,128)S(1)}, u32[]{:S(2)}, u32[]{:S(2)}) async-start(f32[2,64,8]{2,0,1:T(2,128)} %bitcast.15), calls=%async_computation.5 | async-start | bytes 131072 | tf_op jit(solution)/shard_map/all_to_all | solution.py:58
  101.3 12.3 %all-to-all-start.7 = ((f32[2,64,8]{2,0,1:T(2,128)}), f32[2,64,8]{2,0,1:T(2,128)S(1)}, u32[]{:S(2)}, u32[]{:S(2)}) async-start(f32[2,64,8]{2,0,1:T(2,128)} %copy.120), calls=%async_computation.7 | async-start | bytes 131072 | tf_op jit(solution)/shard_map/all_to_all | solution.py:58
  121.6 15.1 %all-to-all-start.8 = ((f32[64,2,8]{2,1,0:T(2,128)}), f32[64,2,8]{2,1,0:T(2,128)S(1)}, u32[]{:S(2)}, u32[]{:S(2)}) async-start(f32[64,2,8]{2,1,0:T(2,128)} %log_add_fusion.10), calls=%async_computation.8 | async-start | bytes 131072 | tf_op jit(solution)/shard_map/all_to_all | solution.py:62
  138.4 17.1 %all-to-all-start.9 = ((f32[8,1,128]{2,1,0:T(1,128)}), f32[8,1,128]{2,1,0:T(1,128)S(1)}, u32[]{:S(2)}, u32[]{:S(2)}) async-start(f32[8,1,128]{2,1,0:T(1,128)} %reshape.82), calls=%async_computation.9 | async-start | bytes 8192 | tf_op jit(solution)/shard_map/all_to_all | solution.py:63
  200.5 13.4 %all-to-all-start.13 = ((f32[8,1,128]{2,1,0:T(1,128)}), f32[8,1,128]{2,1,0:T(1,128)S(1)}, u32[]{:S(2)}, u32[]{:S(2)}) async-start(f32[8,1,128]{2,1,0:T(1,128)} %reshape.86), calls=%async_computation.13 | async-start | bytes 8192 | tf_op jit(solution)/shard_map/all_to_all | solution.py:63
  214.0 11.1 %all-to-all-start.2 = ((f32[8,1,1024]{2,1,0:T(1,128)}), f32[8,1,1024]{2,1,0:T(1,128)S(1)}, u32[]{:S(2)}, u32[]{:S(2)}) async-start(f32[8,1,1024]{2,1,0:T(1,128)} %reshape.74), calls=%async_computation.2 | async-start | bytes 65536 | tf_op jit(solution)/shard_map/all_to_all | solution.py:57
  225.1 13.0 %all-to-all-start.14 = ((f32[8,1,1024]{2,1,0:T(1,128)}), f32[8,1,1024]{2,1,0:T(1,128)S(1)}, u32[]{:S(2)}, u32[]{:S(2)}) async-start(f32[8,1,1024]{2,1,0:T(1,128)} %reshape.88), calls=%async_computation.14 | async-start | bytes 65536 | tf_op jit(solution)/shard_map/all_to_all | solution.py:57
  238.1 11.2 %all-to-all-start.3 = ((f32[32,1,256]{2,1,0:T(1,128)}), f32[32,1,256]{2,1,0:T(1,128)S(1)}, u32[]{:S(2)}, u32[]{:S(2)}) async-start(f32[32,1,256]{2,1,0:T(1,128)} %reshape.76), calls=%async_computation.3 | async-start | bytes 65536 | tf_op jit(solution)/shard_map/all_to_all | solution.py:58
  249.3 13.9 %all-to-all-start.15 = ((f32[32,1,256]{2,1,0:T(1,128)}), f32[32,1,256]{2,1,0:T(1,128)S(1)}, u32[]{:S(2)}, u32[]{:S(2)}) async-start(f32[32,1,256]{2,1,0:T(1,128)} %reshape.90), calls=%async_computation.15 | async-start | bytes 65536 | tf_op jit(solution)/shard_map/all_to_all | solution.py:58
  348.8 29.5 %copy-start = (f32[8,32,256]{2,1,0:T(8,128)S(1)}, f32[8,32,256]{2,1,0:T(8,128)}, u32[]{:S(2)}) copy-start(f32[8,32,256]{2,1,0:T(8,128)} %param.2) | copy-start | bytes 786436
  371.7 13.8 %all-to-all-start.21 = ((f32[8,1,1024]{2,1,0:T(1,128)}), f32[8,1,1024]{2,1,0:T(1,128)S(1)}, u32[]{:S(2)}, u32[]{:S(2)}) async-start(f32[8,1,1024]{2,1,0:T(1,128)} %reshape.102), calls=%async_computation.21 | async-start | bytes 65536 | tf_op jit(solution)/shard_map/all_to_all | solution.py:63
  385.5 22.6 %all-to-all-start = ((f32[8,1,8192]{2,1,0:T(1,128)}), f32[8,1,8192]{2,1,0:T(1,128)S(1)}, u32[]{:S(2)}, u32[]{:S(2)}) async-start(f32[8,1,8192]{2,1,0:T(1,128)} %reshape.70), calls=%async_computation | async-start | bytes 524288 | tf_op jit(solution)/shard_map/all_to_all | solution.py:57
  408.1 17.3 %all-to-all-start.22 = ((f32[8,1,8192]{2,1,0:T(1,128)}), f32[8,1,8192]{2,1,0:T(1,128)S(1)}, u32[]{:S(2)}, u32[]{:S(2)}) async-start(f32[8,1,8192]{2,1,0:T(1,128)} %reshape.104), calls=%async_computation.22 | async-start | bytes 524288 | tf_op jit(solution)/shard_map/all_to_all | solution.py:57
  425.4 37.7 %all-to-all-start.1 = ((f32[32,1,2048]{2,1,0:T(1,128)}), f32[32,1,2048]{2,1,0:T(1,128)S(1)}, u32[]{:S(2)}, u32[]{:S(2)}) async-start(f32[32,1,2048]{2,1,0:T(1,128)} %reshape.72), calls=%async_computation.1 | async-start | bytes 524288 | tf_op jit(solution)/shard_map/all_to_all | solution.py:58
  463.1 15.7 %all-to-all-start.23 = ((f32[32,1,2048]{2,1,0:T(1,128)}), f32[32,1,2048]{2,1,0:T(1,128)S(1)}, u32[]{:S(2)}, u32[]{:S(2)}) async-start(f32[32,1,2048]{2,1,0:T(1,128)} %reshape.106), calls=%async_computation.23 | async-start | bytes 524288 | tf_op jit(solution)/shard_map/all_to_all | solution.py:58
  512.5 35.7 %all-to-all-start.24 = ((f32[32,1,2048]{2,1,0:T(1,128)}), f32[32,1,2048]{2,1,0:T(1,128)S(1)}, u32[]{:S(2)}, u32[]{:S(2)}) async-start(f32[32,1,2048]{2,1,0:T(1,128)} %reshape.108), calls=%async_computation.24 | async-start | bytes 524288 | tf_op jit(solution)/shard_map/all_to_all | solution.py:62
  548.2 15.7 %all-to-all-start.26 = ((f32[32,1,2048]{2,1,0:T(1,128)}), f32[32,1,2048]{2,1,0:T(1,128)S(1)}, u32[]{:S(2)}, u32[]{:S(2)}) async-start(f32[32,1,2048]{2,1,0:T(1,128)} %reshape.112), calls=%async_computation.26 | async-start | bytes 524288 | tf_op jit(solution)/shard_map/all_to_all | solution.py:62
  563.8 42.9 %all-to-all-start.25 = ((f32[8,1,8192]{2,1,0:T(1,128)}), f32[8,1,8192]{2,1,0:T(1,128)S(1)}, u32[]{:S(2)}, u32[]{:S(2)}) async-start(f32[8,1,8192]{2,1,0:T(1,128)} %reshape.110), calls=%async_computation.25 | async-start | bytes 524288 | tf_op jit(solution)/shard_map/all_to_all | solution.py:63
  606.7 17.3 %all-to-all-start.27 = ((f32[8,1,8192]{2,1,0:T(1,128)}), f32[8,1,8192]{2,1,0:T(1,128)S(1)}, u32[]{:S(2)}, u32[]{:S(2)}) async-start(f32[8,1,8192]{2,1,0:T(1,128)} %reshape.114), calls=%async_computation.27 | async-start | bytes 524288 | tf_op jit(solution)/shard_map/all_to_all | solution.py:63
where the time goes:
time: 650 us; the launch traced here: 640 us
  other arithmetic  273 us (42%)
  starting transfers between devices  128 us (20%)
  blocking collectives  87 us (13%)
  local copies, waits for them, and re-layouts  76.4 us (12%)
  waiting for transfers between devices  72.1 us (11%)
    another operation x29, other arithmetic, soft_axis(): lax.reduce_window(values, -jnp.inf, lax.max, tuple(window), (1, 1, 1), tu...  119 us
    add x17, other arithmetic, soft_axis(): return line_max + jnp.log(summed)  44.7 us
    all_to_all x5, starting transfers between devices, backward(): lax.all_to_all(middle, 'py', split_axis=1, concat_axis=2, tiled=True)  39.8 us
    reshape x2, local copies, waits for them, and re-layouts, restrict(): blocks = values.reshape(size_a // 2, 2, size_b // 2, 2, size_c // 2, 2)  36.9 us
    all_to_all x6, starting transfers between devices, forward(): lax.all_to_all(values, 'py', split_axis=2, concat_axis=1, tiled=True)  35.2 us
    all_to_all x6, starting transfers between devices, forward(): lax.all_to_all(middle, 'px', split_axis=1, concat_axis=0, tiled=True)  33.9 us
    all_to_all x3, blocking collectives, backward(): lax.all_to_all(values, 'px', split_axis=0, concat_axis=1, tiled=True)  31.9 us
    all_to_all x5, waiting for transfers between devices, backward(): lax.all_to_all(middle, 'py', split_axis=1, concat_axis=2, tiled=True)  24.8 us
  transfers between devices with their start and end apart: 20, of which 14 were waited for; matrix products, arithmetic and copies ran while one was open for 29% of the time, Pallas kernels for 0%

commit v1 on v0

v1 whole, which is shorter than its diff:
```python
import math

import jax
import jax.numpy as jnp
from jax import lax
from jax.experimental import pallas as pl
from jax.experimental.pallas import tpu as pltpu
from jax.sharding import PartitionSpec as P

LEVELS = 3
BAND = 16
NEG = -1e30
LOG2E = 1.4426950408889634
LN2 = 0.6931471805599453
MESH = pl.DeviceIdType.MESH
HIGHEST = lax.Precision.HIGHEST


def taps_of(level):
    inverse_width = 2.0 ** (LEVELS - 1 - level) / 18.0
    return [math.exp(-float(d * d) * inverse_width) for d in range(BAND + 1)]


def coarse_taps(level):
    taps = taps_of(level)
    weights = []
    for s in range(2):
        weights.append(
            [
                sum(taps[abs(2 * D + u - s)] for u in range(2) if abs(2 * D + u - s) <= BAND)
                for D in range(-BAND // 2, BAND // 2 + 1)
            ]
        )
    return weights


def lane_lo(shape):
    return lax.broadcasted_iota(jnp.int32, shape, 1) < 64


def half(v):
    return pltpu.roll(v, 64, 1)


def mix(a, b):
    lo = lane_lo(a.shape)
    return jnp.where(lo, a, half(b)), jnp.where(lo, half(a), b)


def tree(op, xs):
    xs = list(xs)
    while len(xs) > 1:
        xs = [op(xs[i], xs[i + 1]) if i + 1 < len(xs) else xs[i] for i in range(0, len(xs), 2)]
    return xs[0]


def soft_rows(pad, planes, n, level, store, chunk=16):
    taps = taps_of(level)
    per = n // chunk

    def body(it, carry):
        p = it // per
        c = pl.multiple_of((it % per) * chunk, chunk)

        def tap(d):
            return pad[p, pl.ds(c + d, chunk), :]

        m = tree(jnp.maximum, [tap(d) for d in range(2 * BAND + 1)])
        parts = [jnp.exp2(tap(BAND) - m)]
        for d in range(1, BAND + 1):
            pair = jnp.exp2(tap(BAND - d) - m) + jnp.exp2(tap(BAND + d) - m)
            parts.append(taps[d] * pair)
        accs = [tree(jnp.add, parts[i::4]) for i in range(4)]
        total = (accs[0] + accs[1]) + (accs[2] + accs[3])
        store(p, c, m + jnp.log2(total))
        return carry

    lax.fori_loop(0, planes * per, body, 0)


def soft_rows_copied(pad, planes, first, n, level, store, chunk=16):
    weights = coarse_taps(level)
    per = n // chunk

    def body(it, carry):
        p = it // per
        c = pl.multiple_of((it % per) * chunk, chunk)

        def tap(t):
            return pad[p, pl.ds(first + c + BAND // 2 + t, chunk), :]

        m = tree(jnp.maximum, [tap(t) for t in range(BAND + 1)])
        es = [jnp.exp2(tap(t) - m) for t in range(BAND + 1)]
        for s in range(2):
            total = tree(jnp.add, [weights[s][t] * es[t] for t in range(BAND + 1)])
            store(p, c, s, m + jnp.log2(total))
        return carry

    lax.fori_loop(0, planes * per, body, 0)


def border(pad, n):
    planes, _, lanes = pad.shape
    for p in range(planes):
        pad[p, pl.ds(0, BAND), :] = jnp.full((BAND, lanes), NEG, jnp.float32)
        pad[p, pl.ds(BAND + n, BAND), :] = jnp.full((BAND, lanes), NEG, jnp.float32)


def pair_max(v, axis):
    n = v.shape[axis]
    even = lax.broadcasted_iota(jnp.int32, v.shape, axis) % 2 == 0
    other = jnp.where(even, pltpu.roll(v, n - 1, axis), pltpu.roll(v, 1, axis))
    return jnp.maximum(v, other)


def halving(rows, cols, axis, shift=0):
    i = lax.broadcasted_iota(jnp.int32, (rows, cols), 0)
    j = lax.broadcasted_iota(jnp.int32, (rows, cols), 1)
    if axis == 0:
        return (j // 2 == i).astype(jnp.float32)
    return (i // 2 + shift == j).astype(jnp.float32)


def mm(a, b):
    return jnp.dot(a, b, precision=HIGHEST, preferred_element_type=jnp.float32)


def weight_log(pos, level, n):
    taps = taps_of(level)
    total = jnp.zeros(pos.shape, jnp.float32)
    for d in range(-BAND, BAND + 1):
        inside = (pos + d >= 0) & (pos + d < n)
        total = total + jnp.where(inside, taps[abs(d)], 0.0)
    return jnp.log2(total)


ROUNDS = [
    "g0", "g1", "s2a", "s2b", "x0", "l0a", "l0b", "l0c", "x1", "l1p", "l1a", "l1b", "l1c",
    "l2p", "l2a", "l2b", "fa", "fb",
]


def kernel(src, tgt, f_out, g_out, *scratch):
    names = [name for name, _ in SCRATCH]
    ref = dict(zip(names, scratch))
    send_sem, recv_sem = scratch[-2], scratch[-1]
    px = lax.axis_index("px")
    py = lax.axis_index("py")
    zh = py // 2
    core = py % 2
    g = 2 * px + core

    barrier = pltpu.get_barrier_semaphore()

    def in_group(q):
        return (q // 2, 2 * zh + q % 2)

    def greet_group(o, carry):
        pl.semaphore_signal(barrier, inc=1, device_id=in_group((g + o) % 64), device_id_type=MESH)
        return carry

    def greet_column(o, carry):
        peer = (2 * ((zh + o // 2) % 4)) + o % 2
        pl.semaphore_signal(barrier, inc=1, device_id=(px, peer), device_id_type=MESH)
        return carry

    lax.fori_loop(1, 64, greet_group, 0)
    lax.fori_loop(2, 8, greet_column, 0)

    def exchange(name, n, me, device, src_at, dst_at):
        k = ROUNDS.index(name)

        def one(o, carry):
            q = (me + o) % n
            pltpu.make_async_remote_copy(
                src_ref=src_at(q),
                dst_ref=dst_at(me),
                send_sem=send_sem.at[k],
                recv_sem=recv_sem.at[k],
                device_id=device(q),
                device_id_type=MESH,
            ).start()
            return carry

        lax.fori_loop(1, n, one, 0)
        pltpu.make_async_copy(src_at(me), dst_at(me), recv_sem.at[k]).start()

    def arrived(name, whole):
        k = ROUNDS.index(name)
        pltpu.make_async_copy(whole, whole, recv_sem.at[k]).wait()

    def sent(name, part):
        k = ROUNDS.index(name)
        pltpu.make_async_copy(part, part, send_sem.at[k]).wait()

    def column(q):
        return (px, q)

    def pencil(q):
        return (q, py)

    def depth(q):
        return (px, 2 * q + core)

    es, ms = [], []
    for arr in (src, tgt):
        for d in range(4):
            a = arr[2 * d] * LOG2E
            b = arr[2 * d + 1] * LOG2E
            m = pair_max(pair_max(jnp.maximum(a, b), 0), 1)
            es.append(jnp.exp2(a - m) + jnp.exp2(b - m))
            ms.append(m)
    fine = mm(jnp.concatenate(es + ms, axis=0), halving(256, 128, 1))
    rows = halving(128, 256, 0)
    r1 = mm(rows, fine[256:]) * 0.25 + jnp.log2(mm(rows, fine[:256])) - 3.0
    s1 = ref["g1s"]
    for i in range(8):
        s1[i // 4, i % 4] = r1[16 * i : 16 * i + 16]
    es, ms = [], []
    for d in range(2):
        for arr in range(2):
            o = (arr * 4 + 2 * d) * 16
            a, b = r1[o : o + 16], r1[o + 16 : o + 32]
            m = pair_max(pair_max(jnp.maximum(a, b), 0), 1)
            es.append(jnp.exp2(a - m) + jnp.exp2(b - m))
            ms.append(m)

    def packed(v):
        low = mm(jnp.concatenate(v[:2], axis=0), halving(128, 128, 1))
        high = mm(jnp.concatenate(v[2:], axis=0), halving(128, 128, 1, 64))
        return mm(halving(16, 32, 0), low + high)

    r0 = packed(ms) * 0.25 + jnp.log2(packed(es)) - 3.0
    s0 = ref["g0s"]
    s0[0] = r0[:8]
    s0[1] = r0[8:]

    pl.semaphore_wait(barrier, 69)

    r_g0, r_g1, r_s2a = ref["g0r"], ref["g1r"], ref["s2ar"]
    exchange("g0", 8, py, column, lambda q: s0, lambda q: r_g0.at[q])
    exchange("g1", 8, py, column, lambda q: s1.at[:, pl.ds(2 * (q % 2), 2)], lambda q: r_g1.at[q])
    exchange("s2a", 32, px, pencil, lambda q: src.at[:, q], lambda q: r_s2a.at[pl.ds(8 * q, 8)])

    for name, n in (("m0", 64), ("t0", 64), ("r0", 64), ("m1", 128), ("t1", 128), ("r1", 128), ("c1", 64), ("u2", 128),
                    ("c2", 128), ("m2", 256), ("r2", 256), ("k2", 256)):
        border(ref[name], n)

    m0, t0, q0, w0 = ref["m0"], ref["t0"], ref["r0"], ref["w0"]

    lanes0 = lax.broadcasted_iota(jnp.int32, (64, 128), 1)
    zero0 = (
        weight_log(lax.broadcasted_iota(jnp.int32, (64, 128), 0), 0, 64)
        + weight_log(lanes0 % 64, 0, 64)
        + weight_log(2 * px + lanes0 // 64, 0, 64)
    )

    def turn0(v):
        t = jnp.concatenate([v, v], axis=0).T
        return jnp.where(lane_lo((64, 128)), t[:64], t[64:])

    def scatter0(r, store):
        a, b = mix(r[pl.ds(0, 32, stride=2), :], r[pl.ds(1, 32, stride=2), :])
        store(0, a)
        store(1, b)

    arrived("g0", r_g0)
    x0s, x0r, a0, b0 = ref["x0s"], ref["x0r"], ref["a0"], ref["b0"]
    for i in range(8):
        x0s[8 * i : 8 * i + 8, :] = r_g0[i, 0]
        b0[8 * i : 8 * i + 8, :] = r_g0[i, 1]

    def swap0(name, s, r):
        exchange(name, 32, px, pencil, lambda q: s.at[pl.ds(2 * q, 2)], lambda q: r.at[pl.ds(2 * q, 2)])

    swap0("x0", x0s, x0r)
    arrived("x0", x0r)

    def put_a0(k, v):
        a0[pl.ds(k, 32, stride=2), :] = v

    scatter0(x0r, put_a0)
    m0[0, pl.ds(BAND, 64), :] = a0[...] - zero0

    def transform0(name, other, background):
        s, r = ref[name + "s"], ref[name + "r"]

        def put_w(p, c, v):
            w0[pl.ds(c, 16), :] = v

        soft_rows(m0, 1, 64, 0, put_w)
        t0[0, pl.ds(BAND, 64), :] = turn0(w0[...])
        soft_rows(t0, 1, 64, 0, put_w)
        s[...] = turn0(w0[...])
        swap0(name, s, r)
        background()
        arrived(name, r)

        def put_r(k, v):
            q0[0, pl.ds(BAND + k, 32, stride=2), :] = v

        scatter0(r, put_r)

        def finish(p, c, v):
            m0[0, pl.ds(BAND + c, 16), :] = other[pl.ds(c, 16), :] - v

        soft_rows(q0, 1, 64, 0, finish)

    m1, t1, q1, w1 = ref["m1"], ref["t1"], ref["r1"], ref["w1"]
    a1, b1 = ref["a1"], ref["b1"]

    def swap1(name, s, r):
        exchange(name, 64, g, in_group, lambda q: s.at[pl.ds(4 * q, 4)], lambda q: r.at[pl.ds(4 * q, 4)])

    def gather1(plane_rows, s):
        for a in range(2):
            for b in range(2):
                s[pl.ds(2 * b + a, 64, stride=4), :] = plane_rows(a, b)

    def scatter1(r, store):
        for a in range(2):
            for b in range(2):
                store(b, a, r[pl.ds(2 * b + a, 64, stride=4), :])

    def source1_out():
        arrived("g1", r_g1)
        for i in range(8):
            for a in range(2):
                w1[a, 16 * i : 16 * i + 16, :] = r_g1[i, 0, a]
                b1[a, 16 * i : 16 * i + 16, :] = r_g1[i, 1, a]
        gather1(lambda a, b: w1[a, pl.ds(b, 64, stride=2), :], ref["x1s"])
        swap1("x1", ref["x1s"], ref["x1r"])

    def source2_out():
        arrived("s2a", r_s2a)
        out = ref["s2bs"]
        for pair in range(2):
            cols = slice(128 * pair, 128 * pair + 128)
            a, b = mix(r_s2a[0:128, cols], r_s2a[128:256, cols])
            out[2 * pair] = a
            out[2 * pair + 1] = b
        exchange("s2b", 4, zh, depth, lambda q: out.at[q], lambda q: ref["s2br"].at[q])

    def source1_in():
        arrived("x1", ref["x1r"])

        def put(b, a, v):
            a1[b, pl.ds(a, 64, stride=2), :] = v

        scatter1(ref["x1r"], put)

    transform0("l0a", b0, source1_out)
    transform0("l0b", a0, source2_out)
    transform0("l0c", b0, source1_in)

    g0 = m0[0, pl.ds(BAND, 64), :] * 2.0
    own = jnp.where(core == 0, g0, half(g0))
    c1, u1 = ref["c1"], ref["u1"]
    c1[0, pl.ds(BAND, 64), :] = own

    def put_u(p, c, s, v):
        u1[pl.ds(2 * c + s, 16, stride=2), :] = v

    soft_rows_copied(c1, 1, 0, 64, 1, put_u)
    c1[0, pl.ds(BAND, 64), :] = u1[...].T[:64]
    soft_rows_copied(c1, 1, 0, 64, 1, put_u)
    l1ps, l1pr = ref["l1ps"], ref["l1pr"]
    l1ps[...] = u1[...].T
    exchange("l1p", 64, g, in_group, lambda q: l1ps.at[pl.ds(2 * q, 2)], lambda q: l1pr.at[pl.ds(2 * q, 2)])
    arrived("l1p", l1pr)

    def finish_l1p(b):
        def put(p, c, s, v):
            m1[b, pl.ds(BAND + 2 * c + s, 16, stride=2), :] = a1[b, pl.ds(2 * c + s, 16, stride=2), :] - v

        return put

    for b in range(2):
        c1[0, pl.ds(BAND, 64), :] = l1pr[pl.ds(b, 64, stride=2), :]
        soft_rows_copied(c1, 1, 0, 64, 1, finish_l1p(b))

    def transform1(name, other, background):
        s, r = ref[name + "s"], ref[name + "r"]

        def put_w(p, c, v):
            w1[p, pl.ds(c, 16), :] = v

        soft_rows(m1, 2, 128, 1, put_w)
        for p in range(2):
            t1[p, pl.ds(BAND, 128), :] = w1[p].T
        soft_rows(t1, 2, 128, 1, put_w)
        for p in range(2):
            w1[p] = w1[p].T
        gather1(lambda a, b: w1[a, pl.ds(b, 64, stride=2), :], s)
        swap1(name, s, r)
        background()
        arrived(name, r)

        def put_r(b, a, v):
            q1[b, pl.ds(BAND + a, 64, stride=2), :] = v

        scatter1(r, put_r)

        def finish(p, c, v):
            m1[p, pl.ds(BAND + c, 16), :] = other[p, pl.ds(c, 16), :] - v

        soft_rows(q1, 2, 128, 1, finish)

    a2 = ref["a2"]

    def source2_in():
        arrived("s2b", ref["s2br"])
        r = ref["s2br"]
        for zp in range(2):
            a, b = mix(r[2 * zp], r[2 * zp + 1])
            a2[zp, 0:128, :] = a * LOG2E
            a2[zp, 128:256, :] = b * LOG2E

    transform1("l1a", b1, source2_in)
    transform1("l1b", a1, lambda: None)
    transform1("l1c", b1, lambda: None)

    u2, w2, l2ps, l2pr = ref["u2"], ref["w2"], ref["l2ps"], ref["l2pr"]
    for a in range(2):
        t1[a, pl.ds(BAND, 128), :] = m1[a, pl.ds(BAND, 128), :].T * 2.0

    def put_w2(p, c, s, v):
        w2[pl.ds(64 * p + 2 * c + s, 16, stride=2), :] = v

    soft_rows_copied(t1, 2, pl.multiple_of(32 * zh, 32), 32, 2, put_w2)
    u2[0, pl.ds(BAND, 128), :] = w2[...].T

    def put_l2p(p, c, s, v):
        l2ps[c // 32, pl.ds(2 * (c % 32) + s, 16, stride=2), :] = v

    soft_rows_copied(u2, 1, 0, 128, 2, put_l2p)
    exchange(
        "l2p", 64, g, in_group,
        lambda q: l2ps.at[:, pl.ds(32 * (q % 2) + q // 2, 1)],
        lambda q: l2pr.at[:, pl.ds(q, 1)],
    )
    arrived("l2p", l2pr)
    c2, m2 = ref["c2"], ref["m2"]
    for zp in range(2):
        a, b = mix(l2pr[2 * zp], l2pr[2 * zp + 1])
        c2[zp, pl.ds(BAND, 64, stride=2), :] = a
        c2[zp, pl.ds(BAND + 1, 64, stride=2), :] = b

    def put_m2(p, c, s, v):
        m2[p, pl.ds(BAND + 2 * c + s, 16, stride=2), :] = a2[p, pl.ds(2 * c + s, 16, stride=2), :] - v

    soft_rows_copied(c2, 2, 0, 128, 2, put_m2)

    scale = 0.05 * LN2
    fas, far = ref["fas"], ref["far"]
    for zp in range(2):
        a, b = mix(m2[zp, pl.ds(BAND, 128), :], m2[zp, pl.ds(BAND + 128, 128), :])
        fas[2 * zp] = a * scale
        fas[2 * zp + 1] = b * scale
    exchange("fa", 4, zh, depth, lambda q: fas.at[q], lambda q: far.at[q])

    l2as, l2ar = ref["l2as"], ref["l2ar"]

    def put_l2a(p, c, v):
        l2as[p, pl.ds(c, 16), :] = v

    soft_rows(m2, 2, 256, 2, put_l2a)
    slot = 32 * core + px
    k2a = ROUNDS.index("l2a")

    def send_l2a(o, carry):
        q = (g + o) % 64
        pltpu.make_async_remote_copy(
            src_ref=l2as.at[:, pl.ds(4 * q, 4)],
            dst_ref=l2ar.at[:, pl.ds(4 * slot, 4)],
            send_sem=send_sem.at[k2a],
            recv_sem=recv_sem.at[k2a],
            device_id=in_group(q),
            device_id_type=MESH,
        ).start()
        return carry

    lax.fori_loop(1, 64, send_l2a, 0)
    pltpu.make_async_copy(l2as.at[:, pl.ds(4 * g, 4)], l2ar.at[:, pl.ds(4 * slot, 4)], recv_sem.at[k2a]).start()

    arrived("fa", far)
    fbs, fbr = ref["fbs"], ref["fbr"]
    for pair in range(2):
        a, b = mix(far[2 * pair], far[2 * pair + 1])
        fbs[pair, 0:128, :] = a
        fbs[pair, 128:256, :] = b
    arrived("l2a", l2ar)
    exchange("fb", 32, px, pencil, lambda q: fbs.at[:, pl.ds(8 * q, 8)], lambda q: fbr.at[:, pl.ds(8 * q, 8)])

    q2, l2bs, l2br = ref["r2"], ref["l2bs"], ref["l2br"]
    for zp in range(2):
        for tp in range(2):
            a, b = mix(
                l2ar[zp, pl.ds(2 * tp, 64, stride=4), :], l2ar[zp, pl.ds(2 * tp + 1, 64, stride=4), :]
            )
            q2[tp, pl.ds(BAND + 128 * zp, 64), :] = a
            q2[tp, pl.ds(BAND + 128 * zp + 64, 64), :] = b

    def put_l2b(p, c, v):
        l2bs[p, pl.ds(c, 16), :] = v

    soft_rows(q2, 2, 256, 2, put_l2b)
    exchange("l2b", 8, py, column, lambda q: l2bs.at[:, pl.ds(32 * q, 32)], lambda q: l2br.at[q])
    arrived("fb", fbr)
    for d in range(8):
        for h in range(2):
            f_out[d, :, 128 * h : 128 * h + 128] = fbr[h, pl.ds(d, 32, stride=8), :]
    arrived("l2b", l2br)
    k2, w3 = ref["k2"], ref["w3"]
    for z in range(4):
        t = l2br[2 * z : 2 * z + 2].reshape(128, 128).T
        for tt in range(2):
            k2[tt, pl.ds(BAND + 64 * z, 64), :] = t[64 * tt : 64 * tt + 64]

    def put_w3(p, c, v):
        w3[p, pl.ds(c, 16), :] = v

    soft_rows(k2, 2, 256, 2, put_w3)
    for tt in range(2):
        for h in range(2):
            t = w3[tt, 128 * h : 128 * h + 128, :].T
            for c in range(4):
                cols = slice(128 * h, 128 * h + 128)
                g_out[2 * c + tt, :, cols] = tgt[2 * c + tt, :, cols] * 0.05 - t[32 * c : 32 * c + 32] * scale

    sent("g0", r_g0.at[pl.ds(0, 7)])
    sent("g1", r_g1.at[pl.ds(0, 7)])
    sent("s2a", r_s2a.at[pl.ds(0, 248)])
    sent("s2b", ref["s2br"].at[pl.ds(0, 3)])
    for name in ("x0", "l0a", "l0b", "l0c"):
        sent(name, ref[name + "r"].at[pl.ds(0, 62)])
    for name in ("x1", "l1a", "l1b", "l1c"):
        sent(name, ref[name + "r"].at[pl.ds(0, 252)])
    sent("l1p", l1pr.at[pl.ds(0, 126)])
    sent("l2p", l2pr.at[:, pl.ds(0, 63)])
    sent("l2a", l2ar.at[:, pl.ds(0, 252)])
    sent("l2b", l2br.at[pl.ds(0, 7)])
    sent("fa", far.at[pl.ds(0, 3)])
    sent("fb", fbr.at[:, pl.ds(0, 248)])


SCRATCH = [
    ("g0s", (2, 8, 128)), ("g0r", (8, 2, 8, 128)),
    ("g1s", (2, 4, 16, 128)), ("g1r", (8, 2, 2, 16, 128)),
    ("s2ar", (256, 256)), ("s2bs", (4, 128, 128)), ("s2br", (4, 128, 128)),
    ("x0s", (64, 128)), ("x0r", (64, 128)),
    ("l0as", (64, 128)), ("l0ar", (64, 128)), ("l0bs", (64, 128)), ("l0br", (64, 128)),
    ("l0cs", (64, 128)), ("l0cr", (64, 128)),
    ("x1s", (256, 128)), ("x1r", (256, 128)),
    ("l1ps", (128, 128)), ("l1pr", (128, 128)),
    ("l1as", (256, 128)), ("l1ar", (256, 128)), ("l1bs", (256, 128)), ("l1br", (256, 128)),
    ("l1cs", (256, 128)), ("l1cr", (256, 128)),
    ("l2ps", (4, 64, 128)), ("l2pr", (4, 64, 128)),
    ("l2as", (2, 256, 128)), ("l2ar", (2, 256, 128)),
    ("l2bs", (2, 256, 128)), ("l2br", (8, 2, 32, 128)),
    ("fas", (4, 128, 128)), ("far", (4, 128, 128)), ("fbs", (2, 256, 128)), ("fbr", (2, 256, 128)),
    ("m0", (1, 96, 128)), ("t0", (1, 96, 128)), ("r0", (1, 96, 128)), ("w0", (64, 128)),
    ("a0", (64, 128)), ("b0", (64, 128)),
    ("m1", (2, 160, 128)), ("t1", (2, 160, 128)), ("r1", (2, 160, 128)), ("w1", (2, 128, 128)),
    ("a1", (2, 128, 128)), ("b1", (2, 128, 128)),
    ("c1", (1, 96, 128)), ("u1", (128, 128)),
    ("u2", (1, 160, 128)), ("w2", (128, 128)), ("c2", (2, 160, 128)), ("a2", (2, 256, 128)),
    ("m2", (2, 288, 128)), ("r2", (2, 288, 128)), ("k2", (2, 288, 128)), ("w3", (2, 256, 128)),
]


def per_device(log_source, log_target):
    shape = jax.ShapeDtypeStruct((8, 32, 256), jnp.float32)
    vmem = pl.BlockSpec(memory_space=pltpu.VMEM)
    return pl.pallas_call(
        kernel,
        out_shape=(shape, shape),
        in_specs=[vmem, vmem],
        out_specs=(vmem, vmem),
        scratch_shapes=[pltpu.VMEM(s, jnp.float32) for _, s in SCRATCH]
        + [pltpu.SemaphoreType.DMA((len(ROUNDS),)), pltpu.SemaphoreType.DMA((len(ROUNDS),))],
        compiler_params=pltpu.CompilerParams(collective_id=0, has_side_effects=True),
        name="sinkhorn",
    )(log_source, log_target)


def solution(mesh):
    return jax.shard_map(
        per_device,
        mesh=mesh,
        in_specs=(P("px", "py", None), P("px", "py", None)),
        out_specs=(P("px", "py", None), P("px", "py", None)),
        check_vma=False,
    )
```

time: 650 us -> 118 us (0.18); the launches traced: 640 us -> 118 us
  other arithmetic: 273 us -> 0 us
  starting transfers between devices: 128 us -> 0 us
  Pallas kernels: 0 us -> 115 us
  blocking collectives: 87 us -> 0 us
  local copies, waits for them, and re-layouts: 76.4 us -> 2.42 us
  waiting for transfers between devices: 72.1 us -> 0 us
    all_to_all x20 -> x0, starting transfers between devices: 128 us -> none  [the longest x5 39.8 us: backward(): lax.all_to_all(middle, 'py', split_axis=1, concat_axis=2, tiled=True)]
    another operation x29 -> x0, other arithmetic: 119 us -> none  [soft_axis(): lax.reduce_window(values, -jnp.inf, lax.max, tuple(window), (1, 1, 1), tu...]
    pallas_call x0 -> x1, Pallas kernels: none -> 115 us  [per_device(): pl.pallas_call(kernel, out_shape=(shape, shape), in_specs=[vmem, vmem], o...]
    all_to_all x8 -> x0, blocking collectives: 87 us -> none  [the longest x3 31.9 us: backward(): lax.all_to_all(values, 'px', split_axis=0, concat_axis=1, tiled=True)]
    all_to_all x20 -> x0, waiting for transfers between devices: 72.1 us -> none  [the longest x5 24.8 us: backward(): lax.all_to_all(middle, 'py', split_axis=1, concat_axis=2, tiled=True)]
    add x20 -> x0, other arithmetic: 44.8 us -> none  [the longest x17 44.7 us: soft_axis(): return line_max + jnp.log(summed)]
    reshape x2 -> x0, local copies, waits for them, and re-layouts: 36.9 us -> none  [restrict(): blocks = values.reshape(size_a // 2, 2, size_b // 2, 2, size_c // 2, 2)]
    unnamed x2 -> x0, other arithmetic: 23.5 us -> none
  transfers between devices with their start and end apart: 20 -> 0, of which waited for: 14 -> 0; matrix products, arithmetic and copies ran while one was open for 29% -> 0% of each run, Pallas kernels for 0% -> 0%
where the time goes in v1:
time: 118 us
  Pallas kernels  115 us (97%)
  local copies, waits for them, and re-layouts  2.42 us (2%)
    pallas_call x1, Pallas kernels, per_device(): pl.pallas_call(kernel, out_shape=(shape, shape), in_specs=[vmem, vmem], o...  115 us
    unnamed x4, local copies, waits for them, and re-layouts  2.42 us

profile of v1, /device:TPU:1, one launch (start us, length us, event | category | flops | bytes accessed | tf_op | source)
XLA Modules:
  0.0 118.0 jit_solution(1951121525265696404)
XLA Ops:
  0.6 115.0 %sinkhorn.1 = (f32[8,32,256]{2,1,0:T(8,128)}, f32[8,32,256]{2,1,0:T(8,128)}) custom-call(f32[8,32,256]{2,1,0:T(8,128)} %src.1, f32[8,32,256]{2,1,0:T(8,128)} %tgt.1), custom_call_target="tpu_custom_call" | custom-call | tf_op jit(solution)/shard_map/sinkhorn/pallas_call | solution.py:575
  115.6 0.0 copy-start
  115.6 1.7 %copy.6 = f32[8,32,256]{2,1,0:T(8,128)} copy(f32[8,32,256]{2,1,0:T(8,128)} %get-tuple-element.4) | data formatting | bytes 524288
  117.3 0.0 copy-done
  117.3 0.7 copy.7
Async XLA Ops:
  115.6 1.7 %copy-start = (f32[8,32,256]{2,1,0:T(8,128)S(1)}, f32[8,32,256]{2,1,0:T(8,128)}, u32[]{:S(2)}) copy-start(f32[8,32,256]{2,1,0:T(8,128)} %get-tuple-element.5) | copy-start | bytes 786436

commit v2 on v1

--- a/solution.py
+++ b/solution.py
@@ -99,6 +99,31 @@
     lax.fori_loop(0, planes * per, body, 0)
 
 
+def soft_major(buf, n, level, store, rows=2):
+    taps = taps_of(level)
+    per = n // rows
+
+    def body(it, carry):
+        h = it // per
+        c = (it % per) * rows
+        for r in range(rows):
+
+            def tap(d):
+                return buf[c + r + d, h]
+
+            m = tree(jnp.maximum, [tap(d) for d in range(2 * BAND + 1)])
+            parts = [jnp.exp2(tap(BAND) - m)]
+            for d in range(1, BAND + 1):
+                pair = jnp.exp2(tap(BAND - d) - m) + jnp.exp2(tap(BAND + d) - m)
+                parts.append(taps[d] * pair)
+            accs = [tree(jnp.add, parts[i::4]) for i in range(4)]
+            total = (accs[0] + accs[1]) + (accs[2] + accs[3])
+            store(c + r, h, m + jnp.log2(total))
+        return carry
+
+    lax.fori_loop(0, 2 * per, body, 0)
+
+
 def border(pad, n):
     planes, _, lanes = pad.shape
     for p in range(planes):
@@ -135,8 +160,8 @@
 
 
 ROUNDS = [
-    "g0", "g1", "s2a", "s2b", "x0", "l0a", "l0b", "l0c", "x1", "l1p", "l1a", "l1b", "l1c",
-    "l2p", "l2a", "l2b", "fa", "fb",
+    "g0", "g1", "s2a", "x0", "l0a", "l0b", "l0c", "x1", "l1p", "l1a", "l1b", "l1c",
+    "l2p", "l2own", "l2up", "l2down", "fb",
 ]
 
 
@@ -167,7 +192,20 @@
     lax.fori_loop(1, 64, greet_group, 0)
     lax.fori_loop(2, 8, greet_column, 0)
 
-    def exchange(name, n, me, device, src_at, dst_at):
+    side = jnp.where(core == 0, py - 1, py + 1)
+    has_side = (side >= 0) & (side < 8)
+
+    @pl.when(has_side)
+    def _():
+        def greet_side(o, carry):
+            pl.semaphore_signal(barrier, inc=1, device_id=((px + o) % 32, side), device_id_type=MESH)
+            return carry
+
+        lax.fori_loop(1, 32, greet_side, 0)
+
+    leaving = []
+
+    def exchange(name, n, me, device, src_at, dst_at, most):
         k = ROUNDS.index(name)
 
         def one(o, carry):
@@ -184,6 +222,7 @@
 
         lax.fori_loop(1, n, one, 0)
         pltpu.make_async_copy(src_at(me), dst_at(me), recv_sem.at[k]).start()
+        leaving.append((name, most))
 
     def arrived(name, whole):
         k = ROUNDS.index(name)
@@ -235,15 +274,13 @@
     s0[0] = r0[:8]
     s0[1] = r0[8:]
 
-    pl.semaphore_wait(barrier, 69)
+    pl.semaphore_wait(barrier, jnp.where(has_side, 100, 69))
 
     r_g0, r_g1, r_s2a = ref["g0r"], ref["g1r"], ref["s2ar"]
-    exchange("g0", 8, py, column, lambda q: s0, lambda q: r_g0.at[q])
-    exchange("g1", 8, py, column, lambda q: s1.at[:, pl.ds(2 * (q % 2), 2)], lambda q: r_g1.at[q])
-    exchange("s2a", 32, px, pencil, lambda q: src.at[:, q], lambda q: r_s2a.at[pl.ds(8 * q, 8)])
+    exchange("g0", 8, py, column, lambda q: s0, lambda q: r_g0.at[q], r_g0.at[pl.ds(0, 7)])
 
     for name, n in (("m0", 64), ("t0", 64), ("r0", 64), ("m1", 128), ("t1", 128), ("r1", 128), ("c1", 64), ("u2", 128),
-                    ("c2", 128), ("m2", 256), ("r2", 256), ("k2", 256)):
+                    ("l2pr", 128), ("m2", 256), ("k2", 256)):
         border(ref[name], n)
 
     m0, t0, q0, w0 = ref["m0"], ref["t0"], ref["r0"], ref["w0"]
@@ -271,9 +308,10 @@
         b0[8 * i : 8 * i + 8, :] = r_g0[i, 1]
 
     def swap0(name, s, r):
-        exchange(name, 32, px, pencil, lambda q: s.at[pl.ds(2 * q, 2)], lambda q: r.at[pl.ds(2 * q, 2)])
+        exchange(name, 32, px, pencil, lambda q: s.at[pl.ds(2 * q, 2)], lambda q: r.at[pl.ds(2 * q, 2)], r.at[pl.ds(0, 62)])
 
     swap0("x0", x0s, x0r)
+    exchange("g1", 8, py, column, lambda q: s1.at[:, pl.ds(2 * (q % 2), 2)], lambda q: r_g1.at[q], r_g1.at[pl.ds(0, 7)])
     arrived("x0", x0r)
 
     def put_a0(k, v):
@@ -310,7 +348,7 @@
     a1, b1 = ref["a1"], ref["b1"]
 
     def swap1(name, s, r):
-        exchange(name, 64, g, in_group, lambda q: s.at[pl.ds(4 * q, 4)], lambda q: r.at[pl.ds(4 * q, 4)])
+        exchange(name, 64, g, in_group, lambda q: s.at[pl.ds(4 * q, 4)], lambda q: r.at[pl.ds(4 * q, 4)], r.at[pl.ds(0, 252)])
 
     def gather1(plane_rows, s):
         for a in range(2):
@@ -332,14 +370,12 @@
         swap1("x1", ref["x1s"], ref["x1r"])
 
     def source2_out():
-        arrived("s2a", r_s2a)
-        out = ref["s2bs"]
-        for pair in range(2):
-            cols = slice(128 * pair, 128 * pair + 128)
-            a, b = mix(r_s2a[0:128, cols], r_s2a[128:256, cols])
-            out[2 * pair] = a
-            out[2 * pair + 1] = b
-        exchange("s2b", 4, zh, depth, lambda q: out.at[q], lambda q: ref["s2br"].at[q])
+        exchange(
+            "s2a", 32, px, pencil,
+            lambda q: src.at[:, q],
+            lambda q: r_s2a.at[pl.ds(8 * q, 8)],
+            r_s2a.at[pl.ds(0, 248)],
+        )
 
     def source1_in():
         arrived("x1", ref["x1r"])
@@ -349,9 +385,9 @@
 
         scatter1(ref["x1r"], put)
 
-    transform0("l0a", b0, source1_out)
-    transform0("l0b", a0, source2_out)
-    transform0("l0c", b0, source1_in)
+    transform0("l0a", b0, source2_out)
+    transform0("l0b", a0, source1_out)
+    transform0("l0c", b0, lambda: None)
 
     g0 = m0[0, pl.ds(BAND, 64), :] * 2.0
     own = jnp.where(core == 0, g0, half(g0))
@@ -366,7 +402,8 @@
     soft_rows_copied(c1, 1, 0, 64, 1, put_u)
     l1ps, l1pr = ref["l1ps"], ref["l1pr"]
     l1ps[...] = u1[...].T
-    exchange("l1p", 64, g, in_group, lambda q: l1ps.at[pl.ds(2 * q, 2)], lambda q: l1pr.at[pl.ds(2 * q, 2)])
+    exchange("l1p", 64, g, in_group, lambda q: l1ps.at[pl.ds(2 * q, 2)], lambda q: l1pr.at[pl.ds(2 * q, 2)], l1pr.at[pl.ds(0, 126)])
+    source1_in()
     arrived("l1p", l1pr)
 
     def finish_l1p(b):
@@ -379,7 +416,7 @@
         c1[0, pl.ds(BAND, 64), :] = l1pr[pl.ds(b, 64, stride=2), :]
         soft_rows_copied(c1, 1, 0, 64, 1, finish_l1p(b))
 
-    def transform1(name, other, background):
+    def transform1(name, other, background, times=1.0):
         s, r = ref[name + "s"], ref[name + "r"]
 
         def put_w(p, c, v):
@@ -402,152 +439,164 @@
         scatter1(r, put_r)
 
         def finish(p, c, v):
-            m1[p, pl.ds(BAND + c, 16), :] = other[p, pl.ds(c, 16), :] - v
+            m1[p, pl.ds(BAND + c, 16), :] = (other[p, pl.ds(c, 16), :] - v) * times
 
         soft_rows(q1, 2, 128, 1, finish)
 
     a2 = ref["a2"]
 
     def source2_in():
-        arrived("s2b", ref["s2br"])
-        r = ref["s2br"]
-        for zp in range(2):
-            a, b = mix(r[2 * zp], r[2 * zp + 1])
-            a2[zp, 0:128, :] = a * LOG2E
-            a2[zp, 128:256, :] = b * LOG2E
+        arrived("s2a", r_s2a)
+        for h in range(2):
+            a2[h] = r_s2a[:, 128 * h : 128 * h + 128] * LOG2E
 
     transform1("l1a", b1, source2_in)
     transform1("l1b", a1, lambda: None)
-    transform1("l1c", b1, lambda: None)
-
-    u2, w2, l2ps, l2pr = ref["u2"], ref["w2"], ref["l2ps"], ref["l2pr"]
-    for a in range(2):
-        t1[a, pl.ds(BAND, 128), :] = m1[a, pl.ds(BAND, 128), :].T * 2.0
+    transform1("l1c", b1, lambda: None, 2.0)
+
+    w2, u2, l2ps, l2pr = ref["w2"], ref["u2"], ref["l2ps"], ref["l2pr"]
 
     def put_w2(p, c, s, v):
         w2[pl.ds(64 * p + 2 * c + s, 16, stride=2), :] = v
 
-    soft_rows_copied(t1, 2, pl.multiple_of(32 * zh, 32), 32, 2, put_w2)
+    soft_rows_copied(m1, 2, pl.multiple_of(32 * zh, 32), 32, 2, put_w2)
     u2[0, pl.ds(BAND, 128), :] = w2[...].T
-
-    def put_l2p(p, c, s, v):
-        l2ps[c // 32, pl.ds(2 * (c % 32) + s, 16, stride=2), :] = v
-
-    soft_rows_copied(u2, 1, 0, 128, 2, put_l2p)
+    w3 = ref["w3"]
+
+    def put_w3(p, c, s, v):
+        w3[0, pl.ds(2 * c + s, 16, stride=2), :] = v
+
+    soft_rows_copied(u2, 1, 0, 128, 2, put_w3)
+    for h in range(2):
+        t = w3[0, 128 * h : 128 * h + 128, :].T
+        for a in range(2):
+            l2ps[h, pl.ds(a, 64, stride=2), :] = t[64 * a : 64 * a + 64]
     exchange(
         "l2p", 64, g, in_group,
-        lambda q: l2ps.at[:, pl.ds(32 * (q % 2) + q // 2, 1)],
-        lambda q: l2pr.at[:, pl.ds(q, 1)],
+        lambda q: l2ps.at[:, pl.ds(2 * (32 * (q % 2) + q // 2), 2)],
+        lambda q: l2pr.at[:, pl.ds(BAND + 2 * q, 2)],
+        l2pr.at[:, pl.ds(0, 126)],
     )
-    arrived("l2p", l2pr)
-    c2, m2 = ref["c2"], ref["m2"]
-    for zp in range(2):
-        a, b = mix(l2pr[2 * zp], l2pr[2 * zp + 1])
-        c2[zp, pl.ds(BAND, 64, stride=2), :] = a
-        c2[zp, pl.ds(BAND + 1, 64, stride=2), :] = b
+    arrived("l2p", l2pr.at[:, pl.ds(BAND, 128)])
+    m2, k2, fbs, fbr = ref["m2"], ref["k2"], ref["fbs"], ref["fbr"]
+    scale = 0.05 * LN2
 
     def put_m2(p, c, s, v):
-        m2[p, pl.ds(BAND + 2 * c + s, 16, stride=2), :] = a2[p, pl.ds(2 * c + s, 16, stride=2), :] - v
-
-    soft_rows_copied(c2, 2, 0, 128, 2, put_m2)
-
-    scale = 0.05 * LN2
-    fas, far = ref["fas"], ref["far"]
-    for zp in range(2):
-        a, b = mix(m2[zp, pl.ds(BAND, 128), :], m2[zp, pl.ds(BAND + 128, 128), :])
-        fas[2 * zp] = a * scale
-        fas[2 * zp + 1] = b * scale
-    exchange("fa", 4, zh, depth, lambda q: fas.at[q], lambda q: far.at[q])
-
-    l2as, l2ar = ref["l2as"], ref["l2ar"]
-
-    def put_l2a(p, c, v):
-        l2as[p, pl.ds(c, 16), :] = v
-
-    soft_rows(m2, 2, 256, 2, put_l2a)
-    slot = 32 * core + px
-    k2a = ROUNDS.index("l2a")
-
-    def send_l2a(o, carry):
-        q = (g + o) % 64
-        pltpu.make_async_remote_copy(
-            src_ref=l2as.at[:, pl.ds(4 * q, 4)],
-            dst_ref=l2ar.at[:, pl.ds(4 * slot, 4)],
-            send_sem=send_sem.at[k2a],
-            recv_sem=recv_sem.at[k2a],
-            device_id=in_group(q),
-            device_id_type=MESH,
-        ).start()
-        return carry
-
-    lax.fori_loop(1, 64, send_l2a, 0)
-    pltpu.make_async_copy(l2as.at[:, pl.ds(4 * g, 4)], l2ar.at[:, pl.ds(4 * slot, 4)], recv_sem.at[k2a]).start()
-
-    arrived("fa", far)
-    fbs, fbr = ref["fbs"], ref["fbr"]
-    for pair in range(2):
-        a, b = mix(far[2 * pair], far[2 * pair + 1])
-        fbs[pair, 0:128, :] = a
-        fbs[pair, 128:256, :] = b
-    arrived("l2a", l2ar)
-    exchange("fb", 32, px, pencil, lambda q: fbs.at[:, pl.ds(8 * q, 8)], lambda q: fbr.at[:, pl.ds(8 * q, 8)])
-
-    q2, l2bs, l2br = ref["r2"], ref["l2bs"], ref["l2br"]
-    for zp in range(2):
-        for tp in range(2):
-            a, b = mix(
-                l2ar[zp, pl.ds(2 * tp, 64, stride=4), :], l2ar[zp, pl.ds(2 * tp + 1, 64, stride=4), :]
-            )
-            q2[tp, pl.ds(BAND + 128 * zp, 64), :] = a
-            q2[tp, pl.ds(BAND + 128 * zp + 64, 64), :] = b
-
-    def put_l2b(p, c, v):
-        l2bs[p, pl.ds(c, 16), :] = v
-
-    soft_rows(q2, 2, 256, 2, put_l2b)
-    exchange("l2b", 8, py, column, lambda q: l2bs.at[:, pl.ds(32 * q, 32)], lambda q: l2br.at[q])
+        v = a2[p, pl.ds(2 * c + s, 16, stride=2), :] - v
+        m2[p, pl.ds(BAND + 2 * c + s, 16, stride=2), :] = v
+        fbs[p, pl.ds(2 * c + s, 16, stride=2), :] = v * scale
+
+    soft_rows_copied(l2pr, 2, 0, 128, 2, put_m2)
+    exchange(
+        "fb", 32, px, pencil,
+        lambda q: fbs.at[:, pl.ds(8 * q, 8)],
+        lambda q: fbr.at[:, pl.ds(8 * q, 8)],
+        fbr.at[:, pl.ds(0, 248)],
+    )
+
+    def put_w(p, c, v):
+        w3[p, pl.ds(c, 16), :] = v
+
+    def turn2(store):
+        for i in range(2):
+            for j in range(2):
+                store(i, j, w3[j, 128 * i : 128 * i + 128, :].T)
+
+    def put_k2(i, j, v):
+        k2[i, pl.ds(BAND + 128 * j, 128), :] = v
+
+    soft_rows(m2, 2, 256, 2, put_w)
+    turn2(put_k2)
+    soft_rows(k2, 2, 256, 2, put_w)
+    l2s, l2r = ref["l2s"], ref["l2r"]
+
+    def put_l2s(i, j, v):
+        l2s[i, 128 * j : 128 * j + 128, :] = v
+
+    turn2(put_l2s)
+
+    low = px < 16
+    beside = jnp.where(low, py - 1, py + 1)
+    has_beside = (beside >= 0) & (beside < 8)
+    exchange(
+        "l2own", 32, px, pencil,
+        lambda q: l2s.at[:, pl.ds(8 * q, 8)],
+        lambda q: l2r.at[BAND + q],
+        l2r.at[pl.ds(0, 31)],
+    )
+    up, down = ROUNDS.index("l2up"), ROUNDS.index("l2down")
+
+    def to_beside(k, place):
+        def one(q, carry):
+            pltpu.make_async_remote_copy(
+                src_ref=l2s.at[:, pl.ds(8 * q, 8)],
+                dst_ref=l2r.at[place],
+                send_sem=send_sem.at[k],
+                recv_sem=recv_sem.at[k],
+                device_id=(q, beside),
+                device_id_type=MESH,
+            ).start()
+            return carry
+
+        lax.fori_loop(0, 32, one, 0)
+
+    @pl.when(has_beside & low)
+    def _():
+        to_beside(down, 48 + px)
+
+    @pl.when(has_beside & jnp.logical_not(low))
+    def _():
+        to_beside(up, px - 16)
+
     arrived("fb", fbr)
     for d in range(8):
         for h in range(2):
             f_out[d, :, 128 * h : 128 * h + 128] = fbr[h, pl.ds(d, 32, stride=8), :]
-    arrived("l2b", l2br)
-    k2, w3 = ref["k2"], ref["w3"]
-    for z in range(4):
-        t = l2br[2 * z : 2 * z + 2].reshape(128, 128).T
-        for tt in range(2):
-            k2[tt, pl.ds(BAND + 64 * z, 64), :] = t[64 * tt : 64 * tt + 64]
-
-    def put_w3(p, c, v):
-        w3[p, pl.ds(c, 16), :] = v
-
-    soft_rows(k2, 2, 256, 2, put_w3)
-    for tt in range(2):
-        for h in range(2):
-            t = w3[tt, 128 * h : 128 * h + 128, :].T
-            for c in range(4):
-                cols = slice(128 * h, 128 * h + 128)
-                g_out[2 * c + tt, :, cols] = tgt[2 * c + tt, :, cols] * 0.05 - t[32 * c : 32 * c + 32] * scale
-
-    sent("g0", r_g0.at[pl.ds(0, 7)])
-    sent("g1", r_g1.at[pl.ds(0, 7)])
-    sent("s2a", r_s2a.at[pl.ds(0, 248)])
-    sent("s2b", ref["s2br"].at[pl.ds(0, 3)])
-    for name in ("x0", "l0a", "l0b", "l0c"):
-        sent(name, ref[name + "r"].at[pl.ds(0, 62)])
-    for name in ("x1", "l1a", "l1b", "l1c"):
-        sent(name, ref[name + "r"].at[pl.ds(0, 252)])
-    sent("l1p", l1pr.at[pl.ds(0, 126)])
-    sent("l2p", l2pr.at[:, pl.ds(0, 63)])
-    sent("l2a", l2ar.at[:, pl.ds(0, 252)])
-    sent("l2b", l2br.at[pl.ds(0, 7)])
-    sent("fa", far.at[pl.ds(0, 3)])
-    sent("fb", fbr.at[:, pl.ds(0, 248)])
+
+    arrived("l2own", l2r.at[pl.ds(BAND, 32)])
+    edge = jnp.full((BAND, 2, 8, 128), NEG, jnp.float32)
+
+    @pl.when(py > 0)
+    def _():
+        arrived("l2up", l2r.at[pl.ds(0, BAND)])
+
+    @pl.when(py == 0)
+    def _():
+        l2r[pl.ds(0, BAND)] = edge
+
+    @pl.when(py < 7)
+    def _():
+        arrived("l2down", l2r.at[pl.ds(48, BAND)])
+
+    @pl.when(py == 7)
+    def _():
+        l2r[pl.ds(48, BAND)] = edge
+
+    def put_rows(r, h, v):
+        w3[h, pl.ds(r, 8, stride=32), :] = v
+
+    soft_major(l2r, 32, 2, put_rows)
+    for h in range(2):
+        cols = slice(128 * h, 128 * h + 128)
+        for d in range(8):
+            g_out[d, :, cols] = tgt[d, :, cols] * 0.05 - w3[h, 32 * d : 32 * d + 32, :] * scale
+
+    @pl.when(has_beside & low)
+    def _():
+        sent("l2down", l2r.at[pl.ds(0, 32)])
+
+    @pl.when(has_beside & jnp.logical_not(low))
+    def _():
+        sent("l2up", l2r.at[pl.ds(0, 32)])
+
+    for name, part in leaving:
+        sent(name, part)
 
 
 SCRATCH = [
     ("g0s", (2, 8, 128)), ("g0r", (8, 2, 8, 128)),
     ("g1s", (2, 4, 16, 128)), ("g1r", (8, 2, 2, 16, 128)),
-    ("s2ar", (256, 256)), ("s2bs", (4, 128, 128)), ("s2br", (4, 128, 128)),
+    ("s2ar", (256, 256)),
     ("x0s", (64, 128)), ("x0r", (64, 128)),
     ("l0as", (64, 128)), ("l0ar", (64, 128)), ("l0bs", (64, 128)), ("l0br", (64, 128)),
     ("l0cs", (64, 128)), ("l0cr", (64, 128)),
@@ -555,17 +604,16 @@
     ("l1ps", (128, 128)), ("l1pr", (128, 128)),
     ("l1as", (256, 128)), ("l1ar", (256, 128)), ("l1bs", (256, 128)), ("l1br", (256, 128)),
     ("l1cs", (256, 128)), ("l1cr", (256, 128)),
-    ("l2ps", (4, 64, 128)), ("l2pr", (4, 64, 128)),
-    ("l2as", (2, 256, 128)), ("l2ar", (2, 256, 128)),
-    ("l2bs", (2, 256, 128)), ("l2br", (8, 2, 32, 128)),
-    ("fas", (4, 128, 128)), ("far", (4, 128, 128)), ("fbs", (2, 256, 128)), ("fbr", (2, 256, 128)),
+    ("l2ps", (2, 128, 128)), ("l2pr", (2, 160, 128)),
+    ("l2s", (2, 256, 128)), ("l2r", (64, 2, 8, 128)),
+    ("fbs", (2, 256, 128)), ("fbr", (2, 256, 128)),
     ("m0", (1, 96, 128)), ("t0", (1, 96, 128)), ("r0", (1, 96, 128)), ("w0", (64, 128)),
     ("a0", (64, 128)), ("b0", (64, 128)),
     ("m1", (2, 160, 128)), ("t1", (2, 160, 128)), ("r1", (2, 160, 128)), ("w1", (2, 128, 128)),
     ("a1", (2, 128, 128)), ("b1", (2, 128, 128)),
     ("c1", (1, 96, 128)), ("u1", (128, 128)),
-    ("u2", (1, 160, 128)), ("w2", (128, 128)), ("c2", (2, 160, 128)), ("a2", (2, 256, 128)),
-    ("m2", (2, 288, 128)), ("r2", (2, 288, 128)), ("k2", (2, 288, 128)), ("w3", (2, 256, 128)),
+    ("u2", (1, 160, 128)), ("w2", (128, 128)), ("a2", (2, 256, 128)),
+    ("m2", (2, 288, 128)), ("k2", (2, 288, 128)), ("w3", (2, 256, 128)),
 ]
 
 

time: 118 us -> 107 us (0.907)
  Pallas kernels: 115 us -> 104 us
    pallas_call x1, Pallas kernels: 115 us -> 104 us  [per_device(): pl.pallas_call(kernel, out_shape=(shape, shape), in_specs=[vmem, vmem], o...]
where the time goes in v2:
time: 107 us
  Pallas kernels  104 us (97%)
  local copies, waits for them, and re-layouts  2.42 us (2%)
    pallas_call x1, Pallas kernels, per_device(): pl.pallas_call(kernel, out_shape=(shape, shape), in_specs=[vmem, vmem], o...  104 us
    unnamed x4, local copies, waits for them, and re-layouts  2.42 us

profile of v2, /device:TPU:1, one launch (start us, length us, event | category | flops | bytes accessed | tf_op | source)
XLA Modules:
  0.0 106.8 jit_solution(17876424229914003150)
XLA Ops:
  0.6 103.7 %sinkhorn.1 = (f32[8,32,256]{2,1,0:T(8,128)}, f32[8,32,256]{2,1,0:T(8,128)}) custom-call(f32[8,32,256]{2,1,0:T(8,128)} %src.1, f32[8,32,256]{2,1,0:T(8,128)} %tgt.1), custom_call_target="tpu_custom_call" | custom-call | tf_op jit(solution)/shard_map/sinkhorn/pallas_call | solution.py:623
  104.4 0.0 copy-start
  104.4 1.7 %copy.6 = f32[8,32,256]{2,1,0:T(8,128)} copy(f32[8,32,256]{2,1,0:T(8,128)} %get-tuple-element.4) | data formatting | bytes 524288
  106.1 0.0 copy-done
  106.1 0.7 copy.7
Async XLA Ops:
  104.4 1.7 %copy-start = (f32[8,32,256]{2,1,0:T(8,128)S(1)}, f32[8,32,256]{2,1,0:T(8,128)}, u32[]{:S(2)}) copy-start(f32[8,32,256]{2,1,0:T(8,128)} %get-tuple-element.5) | copy-start | bytes 786436

commit v3 on v2

--- a/solution.py
+++ b/solution.py
@@ -54,28 +54,44 @@
     return xs[0]
 
 
-def soft_rows(pad, planes, n, level, store, chunk=16):
+def soft_pair(tap, taps):
+    shared = tree(jnp.maximum, [tap(t) for t in range(1, 2 * BAND + 1)])
+    e = {t: jnp.exp2(tap(t) - shared) for t in range(1, 2 * BAND + 1)}
+    outs = []
+    for k in range(2):
+        mid = BAND + k
+        parts = [taps[0] * e[mid]]
+        parts += [taps[d] * (e[mid - d] + e[mid + d]) for d in range(1, BAND)]
+        parts += [taps[BAND] * e[1 if k else 2 * BAND]]
+        accs = [tree(jnp.add, parts[i::4]) for i in range(4)]
+        total = (accs[0] + accs[1]) + (accs[2] + accs[3])
+        last = tap((2 * BAND + 1) * k)
+        m = jnp.maximum(shared, last)
+        total = total * jnp.exp2(shared - m) + taps[BAND] * jnp.exp2(last - m)
+        outs.append(m + jnp.log2(total))
+    return outs
+
+
+def soft_rows(pad, planes, n, level, store, units=4):
     taps = taps_of(level)
-    per = n // chunk
+    size = 16 * units
+    per = n // size
 
     def body(it, carry):
         p = it // per
-        c = pl.multiple_of((it % per) * chunk, chunk)
-
-        def tap(d):
-            return pad[p, pl.ds(c + d, chunk), :]
-
-        m = tree(jnp.maximum, [tap(d) for d in range(2 * BAND + 1)])
-        parts = [jnp.exp2(tap(BAND) - m)]
-        for d in range(1, BAND + 1):
-            pair = jnp.exp2(tap(BAND - d) - m) + jnp.exp2(tap(BAND + d) - m)
-            parts.append(taps[d] * pair)
-        accs = [tree(jnp.add, parts[i::4]) for i in range(4)]
-        total = (accs[0] + accs[1]) + (accs[2] + accs[3])
-        store(p, c, m + jnp.log2(total))
+        base = pl.multiple_of((it % per) * size, size)
+        for u in range(units):
+            c = base + 16 * u
+            outs = soft_pair(lambda t, c=c: pad[p, pl.ds(c + t, 8, stride=2), :], taps)
+            for k in range(2):
+                store(p, c + k, outs[k])
         return carry
 
     lax.fori_loop(0, planes * per, body, 0)
+
+
+def every2(start, count=8):
+    return pl.ds(start, count, stride=2)
 
 
 def soft_rows_copied(pad, planes, first, n, level, store, chunk=16):
@@ -99,26 +115,19 @@
     lax.fori_loop(0, planes * per, body, 0)
 
 
-def soft_major(buf, n, level, store, rows=2):
+def soft_major(buf, n, level, store, units=4):
     taps = taps_of(level)
-    per = n // rows
+    size = 2 * units
+    per = n // size
 
     def body(it, carry):
         h = it // per
-        c = (it % per) * rows
-        for r in range(rows):
-
-            def tap(d):
-                return buf[c + r + d, h]
-
-            m = tree(jnp.maximum, [tap(d) for d in range(2 * BAND + 1)])
-            parts = [jnp.exp2(tap(BAND) - m)]
-            for d in range(1, BAND + 1):
-                pair = jnp.exp2(tap(BAND - d) - m) + jnp.exp2(tap(BAND + d) - m)
-                parts.append(taps[d] * pair)
-            accs = [tree(jnp.add, parts[i::4]) for i in range(4)]
-            total = (accs[0] + accs[1]) + (accs[2] + accs[3])
-            store(c + r, h, m + jnp.log2(total))
+        base = (it % per) * size
+        for u in range(units):
+            c = base + 2 * u
+            outs = soft_pair(lambda t, c=c: buf[c + t, h], taps)
+            for k in range(2):
+                store(c + k, h, outs[k])
         return carry
 
     lax.fori_loop(0, 2 * per, body, 0)
@@ -163,6 +172,12 @@
     "g0", "g1", "s2a", "x0", "l0a", "l0b", "l0c", "x1", "l1p", "l1a", "l1b", "l1c",
     "l2p", "l2own", "l2up", "l2down", "fb",
 ]
+
+
+FAR_FIRST = sorted(
+    [(x, y, z, c) for x in range(4) for y in range(4) for z in range(2) for c in range(2)][1:],
+    key=lambda d: -(min(d[0], 4 - d[0]) + min(d[1], 4 - d[1]) + d[2]),
+)
 
 
 def kernel(src, tgt, f_out, g_out, *scratch):
@@ -180,36 +195,23 @@
     def in_group(q):
         return (q // 2, 2 * zh + q % 2)
 
-    def greet_group(o, carry):
-        pl.semaphore_signal(barrier, inc=1, device_id=in_group((g + o) % 64), device_id_type=MESH)
-        return carry
-
-    def greet_column(o, carry):
-        peer = (2 * ((zh + o // 2) % 4)) + o % 2
-        pl.semaphore_signal(barrier, inc=1, device_id=(px, peer), device_id_type=MESH)
-        return carry
-
-    lax.fori_loop(1, 64, greet_group, 0)
-    lax.fori_loop(2, 8, greet_column, 0)
-
-    side = jnp.where(core == 0, py - 1, py + 1)
-    has_side = (side >= 0) & (side < 8)
-
-    @pl.when(has_side)
-    def _():
-        def greet_side(o, carry):
-            pl.semaphore_signal(barrier, inc=1, device_id=((px + o) % 32, side), device_id_type=MESH)
-            return carry
-
-        lax.fori_loop(1, 32, greet_side, 0)
-
+    for o in range(1, 32):
+        pl.semaphore_signal(barrier, inc=1, device_id=((px + o) % 32, py), device_id_type=MESH)
+    for o in range(1, 8):
+        pl.semaphore_signal(barrier, inc=1, device_id=(px, (py + o) % 8), device_id_type=MESH)
+
+    near = [
+        [(px % 4 + d) % 4 for d in range(4)],
+        [(px // 4 % 4 + d) % 4 for d in range(4)],
+        [(px // 16 + d) % 2 for d in range(2)],
+        [(core + d) % 2 for d in range(2)],
+    ]
     leaving = []
 
     def exchange(name, n, me, device, src_at, dst_at, most):
         k = ROUNDS.index(name)
 
-        def one(o, carry):
-            q = (me + o) % n
+        def to(q):
             pltpu.make_async_remote_copy(
                 src_ref=src_at(q),
                 dst_ref=dst_at(me),
@@ -218,9 +220,16 @@
                 device_id=device(q),
                 device_id_type=MESH,
             ).start()
+
+        def one(o, carry):
+            to((me + o) % n)
             return carry
 
-        lax.fori_loop(1, n, one, 0)
+        if n == 64:
+            for dx, dy, dz, dc in FAR_FIRST:
+                to(2 * (16 * near[2][dz] + 4 * near[1][dy] + near[0][dx]) + near[3][dc])
+        else:
+            lax.fori_loop(1, n, one, 0)
         pltpu.make_async_copy(src_at(me), dst_at(me), recv_sem.at[k]).start()
         leaving.append((name, most))
 
@@ -274,7 +283,7 @@
     s0[0] = r0[:8]
     s0[1] = r0[8:]
 
-    pl.semaphore_wait(barrier, jnp.where(has_side, 100, 69))
+    pl.semaphore_wait(barrier, 38)
 
     r_g0, r_g1, r_s2a = ref["g0r"], ref["g1r"], ref["s2ar"]
     exchange("g0", 8, py, column, lambda q: s0, lambda q: r_g0.at[q], r_g0.at[pl.ds(0, 7)])
@@ -324,7 +333,7 @@
         s, r = ref[name + "s"], ref[name + "r"]
 
         def put_w(p, c, v):
-            w0[pl.ds(c, 16), :] = v
+            w0[every2(c), :] = v
 
         soft_rows(m0, 1, 64, 0, put_w)
         t0[0, pl.ds(BAND, 64), :] = turn0(w0[...])
@@ -340,7 +349,7 @@
         scatter0(r, put_r)
 
         def finish(p, c, v):
-            m0[0, pl.ds(BAND + c, 16), :] = other[pl.ds(c, 16), :] - v
+            m0[0, every2(BAND + c), :] = other[every2(c), :] - v
 
         soft_rows(q0, 1, 64, 0, finish)
 
@@ -348,25 +357,24 @@
     a1, b1 = ref["a1"], ref["b1"]
 
     def swap1(name, s, r):
-        exchange(name, 64, g, in_group, lambda q: s.at[pl.ds(4 * q, 4)], lambda q: r.at[pl.ds(4 * q, 4)], r.at[pl.ds(0, 252)])
-
-    def gather1(plane_rows, s):
-        for a in range(2):
-            for b in range(2):
-                s[pl.ds(2 * b + a, 64, stride=4), :] = plane_rows(a, b)
+        exchange(
+            name, 64, g, in_group,
+            lambda q: s.at[:, pl.ds(2 * q, 2)],
+            lambda q: r.at[:, pl.ds(2 * q, 2)],
+            r.at[:, pl.ds(0, 126)],
+        )
 
     def scatter1(r, store):
         for a in range(2):
             for b in range(2):
-                store(b, a, r[pl.ds(2 * b + a, 64, stride=4), :])
+                store(b, a, r[a, every2(b, 64), :])
 
     def source1_out():
         arrived("g1", r_g1)
         for i in range(8):
             for a in range(2):
-                w1[a, 16 * i : 16 * i + 16, :] = r_g1[i, 0, a]
+                ref["x1s"][a, 16 * i : 16 * i + 16, :] = r_g1[i, 0, a]
                 b1[a, 16 * i : 16 * i + 16, :] = r_g1[i, 1, a]
-        gather1(lambda a, b: w1[a, pl.ds(b, 64, stride=2), :], ref["x1s"])
         swap1("x1", ref["x1s"], ref["x1r"])
 
     def source2_out():
@@ -420,15 +428,14 @@
         s, r = ref[name + "s"], ref[name + "r"]
 
         def put_w(p, c, v):
-            w1[p, pl.ds(c, 16), :] = v
+            w1[p, every2(c), :] = v
 
         soft_rows(m1, 2, 128, 1, put_w)
         for p in range(2):
             t1[p, pl.ds(BAND, 128), :] = w1[p].T
         soft_rows(t1, 2, 128, 1, put_w)
         for p in range(2):
-            w1[p] = w1[p].T
-        gather1(lambda a, b: w1[a, pl.ds(b, 64, stride=2), :], s)
+            s[p] = w1[p].T
         swap1(name, s, r)
         background()
         arrived(name, r)
@@ -439,7 +446,7 @@
         scatter1(r, put_r)
 
         def finish(p, c, v):
-            m1[p, pl.ds(BAND + c, 16), :] = (other[p, pl.ds(c, 16), :] - v) * times
+            m1[p, every2(BAND + c), :] = (other[p, every2(c), :] - v) * times
 
         soft_rows(q1, 2, 128, 1, finish)
 
@@ -495,7 +502,7 @@
     )
 
     def put_w(p, c, v):
-        w3[p, pl.ds(c, 16), :] = v
+        w3[p, every2(c), :] = v
 
     def turn2(store):
         for i in range(2):
@@ -600,10 +607,10 @@
     ("x0s", (64, 128)), ("x0r", (64, 128)),
     ("l0as", (64, 128)), ("l0ar", (64, 128)), ("l0bs", (64, 128)), ("l0br", (64, 128)),
     ("l0cs", (64, 128)), ("l0cr", (64, 128)),
-    ("x1s", (256, 128)), ("x1r", (256, 128)),
+    ("x1s", (2, 128, 128)), ("x1r", (2, 128, 128)),
     ("l1ps", (128, 128)), ("l1pr", (128, 128)),
-    ("l1as", (256, 128)), ("l1ar", (256, 128)), ("l1bs", (256, 128)), ("l1br", (256, 128)),
-    ("l1cs", (256, 128)), ("l1cr", (256, 128)),
+    ("l1as", (2, 128, 128)), ("l1ar", (2, 128, 128)), ("l1bs", (2, 128, 128)), ("l1br", (2, 128, 128)),
+    ("l1cs", (2, 128, 128)), ("l1cr", (2, 128, 128)),
     ("l2ps", (2, 128, 128)), ("l2pr", (2, 160, 128)),
     ("l2s", (2, 256, 128)), ("l2r", (64, 2, 8, 128)),
     ("fbs", (2, 256, 128)), ("fbr", (2, 256, 128)),

time: 107 us -> 92.8 us (0.87)
  Pallas kernels: 104 us -> 89.6 us
    pallas_call x1, Pallas kernels: 104 us -> 89.6 us  [per_device(): pl.pallas_call(kernel, out_shape=(shape, shape), in_specs=[vmem, vmem], o...]
where the time goes in v3:
time: 92.8 us; the launch traced here: 92.6 us
  Pallas kernels  89.6 us (97%)
  local copies, waits for them, and re-layouts  2.42 us (3%)
    pallas_call x1, Pallas kernels, per_device(): pl.pallas_call(kernel, out_shape=(shape, shape), in_specs=[vmem, vmem], o...  89.6 us
    unnamed x4, local copies, waits for them, and re-layouts  2.42 us

profile of v3, /device:TPU:1, one launch (start us, length us, event | category | flops | bytes accessed | tf_op | source)
XLA Modules:
  0.0 92.6 jit_solution(11534612716038549705)
XLA Ops:
  0.6 89.6 %sinkhorn.1 = (f32[8,32,256]{2,1,0:T(8,128)}, f32[8,32,256]{2,1,0:T(8,128)}) custom-call(f32[8,32,256]{2,1,0:T(8,128)} %src.1, f32[8,32,256]{2,1,0:T(8,128)} %tgt.1), custom_call_target="tpu_custom_call" | custom-call | tf_op jit(solution)/shard_map/sinkhorn/pallas_call | solution.py:630
  90.2 0.0 copy-start
  90.2 1.7 %copy.6 = f32[8,32,256]{2,1,0:T(8,128)} copy(f32[8,32,256]{2,1,0:T(8,128)} %get-tuple-element.4) | data formatting | bytes 524288
  91.9 0.0 copy-done
  91.9 0.7 copy.7
Async XLA Ops:
  90.2 1.7 %copy-start = (f32[8,32,256]{2,1,0:T(8,128)S(1)}, f32[8,32,256]{2,1,0:T(8,128)}, u32[]{:S(2)}) copy-start(f32[8,32,256]{2,1,0:T(8,128)} %get-tuple-element.5) | copy-start | bytes 786436

commit v4 on v3

--- a/solution.py
+++ b/solution.py
@@ -1,3 +1,4 @@
+import functools
 import math
 
 import jax
@@ -189,16 +190,29 @@
     zh = py // 2
     core = py % 2
     g = 2 * px + core
+    z = 2 * zh + px // 16
+    own = 16 * core + px % 16
 
     barrier = pltpu.get_barrier_semaphore()
 
     def in_group(q):
         return (q // 2, 2 * zh + q % 2)
 
+    def greet(x, y):
+        pl.semaphore_signal(barrier, inc=1, device_id=(x, y), device_id_type=MESH)
+
     for o in range(1, 32):
-        pl.semaphore_signal(barrier, inc=1, device_id=((px + o) % 32, py), device_id_type=MESH)
+        greet((px + o) % 32, own // 4)
     for o in range(1, 8):
-        pl.semaphore_signal(barrier, inc=1, device_id=(px, (py + o) % 8), device_id_type=MESH)
+        greet(own, (py + o) % 8)
+
+    @pl.when(own // 4 != py)
+    def _():
+        greet(px, own // 4)
+
+    @pl.when(own != px)
+    def _():
+        greet(own, py)
 
     near = [
         [(px % 4 + d) % 4 for d in range(4)],
@@ -225,7 +239,11 @@
             to((me + o) % n)
             return carry
 
-        if n == 64:
+        if device is plane:
+            for dx, dy, dz, dc in FAR_FIRST:
+                if dz == 0:
+                    to(16 * near[3][dc] + 4 * near[1][dy] + near[0][dx])
+        elif n == 64:
             for dx, dy, dz, dc in FAR_FIRST:
                 to(2 * (16 * near[2][dz] + 4 * near[1][dy] + near[0][dx]) + near[3][dc])
         else:
@@ -244,11 +262,11 @@
     def column(q):
         return (px, q)
 
+    def plane(q):
+        return (16 * (px // 16) + q % 16, 2 * zh + q // 16)
+
     def pencil(q):
         return (q, py)
-
-    def depth(q):
-        return (px, 2 * q + core)
 
     es, ms = [], []
     for arr in (src, tgt):
@@ -283,10 +301,47 @@
     s0[0] = r0[:8]
     s0[1] = r0[8:]
 
-    pl.semaphore_wait(barrier, 38)
-
-    r_g0, r_g1, r_s2a = ref["g0r"], ref["g1r"], ref["s2ar"]
-    exchange("g0", 8, py, column, lambda q: s0, lambda q: r_g0.at[q], r_g0.at[pl.ds(0, 7)])
+    own_source = (own // 4 == py).astype(jnp.int32)
+    own_target = (own == px).astype(jnp.int32)
+    pl.semaphore_wait(barrier, 40 - own_source - own_target)
+
+    r_g1, r_s2a = ref["g1r"], ref["s2ar"]
+    x0r, a0, b0 = ref["x0r"], ref["a0"], ref["b0"]
+    k_x0, k_g0 = ROUNDS.index("x0"), ROUNDS.index("g0")
+
+    def first_send(k, part, place, x, y):
+        pltpu.make_async_remote_copy(
+            src_ref=part,
+            dst_ref=place,
+            send_sem=send_sem.at[k],
+            recv_sem=recv_sem.at[k],
+            device_id=(x, y),
+            device_id_type=MESH,
+        ).start()
+
+    def first_own(k, part, place):
+        pltpu.make_async_copy(part, place, recv_sem.at[k]).start()
+
+    for o in (4, 3, 5, 2, 6, 1, 7, 0):
+        to_z = (z + o) % 8
+        for r in range(4):
+            p = 4 * py + r
+            x, y = 16 * (to_z % 2) + p % 16, 2 * (to_z // 2) + p // 16
+            part, place = s0.at[0, pl.ds(2 * r, 2)], x0r.at[pl.ds(2 * px, 2)]
+            if o:
+                first_send(k_x0, part, place, x, y)
+            else:
+                pl.when(p != own)(functools.partial(first_send, k_x0, part, place, x, y))
+                pl.when(p == own)(functools.partial(first_own, k_x0, part, place))
+    for o in (4, 3, 5, 2, 6, 1, 7, 0):
+        to_z = (z + o) % 8
+        x, y = 16 * (to_z % 2) + px % 16, 2 * (to_z // 2) + px // 16
+        part, place = s0.at[1], b0.at[pl.ds(8 * py, 8)]
+        if o:
+            first_send(k_g0, part, place, x, y)
+        else:
+            pl.when(own != px)(functools.partial(first_send, k_g0, part, place, x, y))
+            pl.when(own == px)(functools.partial(first_own, k_g0, part, place))
 
     for name, n in (("m0", 64), ("t0", 64), ("r0", 64), ("m1", 128), ("t1", 128), ("r1", 128), ("c1", 64), ("u2", 128),
                     ("l2pr", 128), ("m2", 256), ("k2", 256)):
@@ -298,7 +353,7 @@
     zero0 = (
         weight_log(lax.broadcasted_iota(jnp.int32, (64, 128), 0), 0, 64)
         + weight_log(lanes0 % 64, 0, 64)
-        + weight_log(2 * px + lanes0 // 64, 0, 64)
+        + weight_log(2 * own + lanes0 // 64, 0, 64)
     )
 
     def turn0(v):
@@ -310,17 +365,14 @@
         store(0, a)
         store(1, b)
 
-    arrived("g0", r_g0)
-    x0s, x0r, a0, b0 = ref["x0s"], ref["x0r"], ref["a0"], ref["b0"]
-    for i in range(8):
-        x0s[8 * i : 8 * i + 8, :] = r_g0[i, 0]
-        b0[8 * i : 8 * i + 8, :] = r_g0[i, 1]
-
     def swap0(name, s, r):
-        exchange(name, 32, px, pencil, lambda q: s.at[pl.ds(2 * q, 2)], lambda q: r.at[pl.ds(2 * q, 2)], r.at[pl.ds(0, 62)])
-
-    swap0("x0", x0s, x0r)
-    exchange("g1", 8, py, column, lambda q: s1.at[:, pl.ds(2 * (q % 2), 2)], lambda q: r_g1.at[q], r_g1.at[pl.ds(0, 7)])
+        exchange(
+            name, 32, own, plane,
+            lambda q: s.at[pl.ds(2 * q, 2)],
+            lambda q: r.at[pl.ds(2 * q, 2)],
+            r.at[pl.ds(0, 62)],
+        )
+
     arrived("x0", x0r)
 
     def put_a0(k, v):
@@ -393,14 +445,24 @@
 
         scatter1(ref["x1r"], put)
 
-    transform0("l0a", b0, source2_out)
+    def first_background():
+        exchange(
+            "g1", 8, py, column,
+            lambda q: s1.at[:, pl.ds(2 * (q % 2), 2)],
+            lambda q: r_g1.at[q],
+            r_g1.at[pl.ds(0, 7)],
+        )
+        source2_out()
+        arrived("g0", b0)
+
+    transform0("l0a", b0, first_background)
     transform0("l0b", a0, source1_out)
     transform0("l0c", b0, lambda: None)
 
     g0 = m0[0, pl.ds(BAND, 64), :] * 2.0
-    own = jnp.where(core == 0, g0, half(g0))
+    mine = jnp.where(px < 16, g0, half(g0))
     c1, u1 = ref["c1"], ref["u1"]
-    c1[0, pl.ds(BAND, 64), :] = own
+    c1[0, pl.ds(BAND, 64), :] = mine
 
     def put_u(p, c, s, v):
         u1[pl.ds(2 * c + s, 16, stride=2), :] = v
@@ -410,7 +472,13 @@
     soft_rows_copied(c1, 1, 0, 64, 1, put_u)
     l1ps, l1pr = ref["l1ps"], ref["l1pr"]
     l1ps[...] = u1[...].T
-    exchange("l1p", 64, g, in_group, lambda q: l1ps.at[pl.ds(2 * q, 2)], lambda q: l1pr.at[pl.ds(2 * q, 2)], l1pr.at[pl.ds(0, 126)])
+    coarse = 2 * own + px // 16
+    exchange(
+        "l1p", 64, g, in_group,
+        lambda q: l1ps.at[pl.ds(2 * q, 2)],
+        lambda q: l1pr.at[pl.ds(2 * coarse, 2)],
+        l1pr.at[pl.ds(0, 126)],
+    )
     source1_in()
     arrived("l1p", l1pr)
 
@@ -598,13 +666,17 @@
 
     for name, part in leaving:
         sent(name, part)
+    sent("x0", x0r.at[pl.ds(0, 62)])
+    sent("g0", b0.at[pl.ds(0, 56)])
+    pl.when(own // 4 != py)(lambda: sent("x0", x0r.at[pl.ds(0, 2)]))
+    pl.when(own != px)(lambda: sent("g0", b0.at[pl.ds(0, 8)]))
 
 
 SCRATCH = [
-    ("g0s", (2, 8, 128)), ("g0r", (8, 2, 8, 128)),
+    ("g0s", (2, 8, 128)),
     ("g1s", (2, 4, 16, 128)), ("g1r", (8, 2, 2, 16, 128)),
     ("s2ar", (256, 256)),
-    ("x0s", (64, 128)), ("x0r", (64, 128)),
+    ("x0r", (64, 128)),
     ("l0as", (64, 128)), ("l0ar", (64, 128)), ("l0bs", (64, 128)), ("l0br", (64, 128)),
     ("l0cs", (64, 128)), ("l0cr", (64, 128)),
     ("x1s", (2, 128, 128)), ("x1r", (2, 128, 128)),

time: 92.8 us -> 87.9 us (0.947)
  Pallas kernels: 89.6 us -> 84.7 us
    pallas_call x1, Pallas kernels: 89.6 us -> 84.7 us  [per_device(): pl.pallas_call(kernel, out_shape=(shape, shape), in_specs=[vmem, vmem], o...]
where the time goes in v4:
time: 87.9 us; the launch traced here: 87.7 us
  Pallas kernels  84.7 us (96%)
  local copies, waits for them, and re-layouts  2.42 us (3%)
    pallas_call x1, Pallas kernels, per_device(): pl.pallas_call(kernel, out_shape=(shape, shape), in_specs=[vmem, vmem], o...  84.7 us
    unnamed x4, local copies, waits for them, and re-layouts  2.42 us

profile of v4, /device:TPU:1, one launch (start us, length us, event | category | flops | bytes accessed | tf_op | source)
XLA Modules:
  0.0 87.7 jit_solution(5829986254377113605)
XLA Ops:
  0.6 84.7 %sinkhorn.1 = (f32[8,32,256]{2,1,0:T(8,128)}, f32[8,32,256]{2,1,0:T(8,128)}) custom-call(f32[8,32,256]{2,1,0:T(8,128)} %src.1, f32[8,32,256]{2,1,0:T(8,128)} %tgt.1), custom_call_target="tpu_custom_call" | custom-call | tf_op jit(solution)/shard_map/sinkhorn/pallas_call | solution.py:702
  85.3 0.0 copy-start
  85.3 1.7 %copy.6 = f32[8,32,256]{2,1,0:T(8,128)} copy(f32[8,32,256]{2,1,0:T(8,128)} %get-tuple-element.4) | data formatting | bytes 524288
  87.0 0.0 copy-done
  87.0 0.7 copy.7
Async XLA Ops:
  85.3 1.7 %copy-start = (f32[8,32,256]{2,1,0:T(8,128)S(1)}, f32[8,32,256]{2,1,0:T(8,128)}, u32[]{:S(2)}) copy-start(f32[8,32,256]{2,1,0:T(8,128)} %get-tuple-element.5) | copy-start | bytes 786436

commit v5 on v4

--- a/solution.py
+++ b/solution.py
@@ -181,10 +181,15 @@
 )
 
 
-def kernel(src, tgt, f_out, g_out, *scratch):
+def kernel(src_in, tgt_in, f_into, g_into, *scratch):
     names = [name for name, _ in SCRATCH]
     ref = dict(zip(names, scratch))
-    send_sem, recv_sem = scratch[-2], scratch[-1]
+    io_sem, send_sem, recv_sem = scratch[-3:]
+    src, tgt, f_out, g_out = ref["src"], ref["tgt"], ref["f"], ref["g"]
+    read_src = pltpu.make_async_copy(src_in, src, io_sem.at[0])
+    read_tgt = pltpu.make_async_copy(tgt_in, tgt, io_sem.at[1])
+    read_src.start()
+    read_tgt.start()
     px = lax.axis_index("px")
     py = lax.axis_index("py")
     zh = py // 2
@@ -268,6 +273,12 @@
     def pencil(q):
         return (q, py)
 
+    for name, n in (("m0", 64), ("t0", 64), ("r0", 64), ("m1", 128), ("t1", 128), ("r1", 128), ("c1", 64), ("u2", 128),
+                    ("l2pr", 128), ("m2", 256), ("k2", 256)):
+        border(ref[name], n)
+
+    read_src.wait()
+    read_tgt.wait()
     es, ms = [], []
     for arr in (src, tgt):
         for d in range(4):
@@ -343,10 +354,6 @@
             pl.when(own != px)(functools.partial(first_send, k_g0, part, place, x, y))
             pl.when(own == px)(functools.partial(first_own, k_g0, part, place))
 
-    for name, n in (("m0", 64), ("t0", 64), ("r0", 64), ("m1", 128), ("t1", 128), ("r1", 128), ("c1", 64), ("u2", 128),
-                    ("l2pr", 128), ("m2", 256), ("k2", 256)):
-        border(ref[name], n)
-
     m0, t0, q0, w0 = ref["m0"], ref["t0"], ref["r0"], ref["w0"]
 
     lanes0 = lax.broadcasted_iota(jnp.int32, (64, 128), 1)
@@ -553,18 +560,15 @@
         l2pr.at[:, pl.ds(0, 126)],
     )
     arrived("l2p", l2pr.at[:, pl.ds(BAND, 128)])
-    m2, k2, fbs, fbr = ref["m2"], ref["k2"], ref["fbs"], ref["fbr"]
-    scale = 0.05 * LN2
+    m2, k2, fbr = ref["m2"], ref["k2"], ref["fbr"]
 
     def put_m2(p, c, s, v):
-        v = a2[p, pl.ds(2 * c + s, 16, stride=2), :] - v
-        m2[p, pl.ds(BAND + 2 * c + s, 16, stride=2), :] = v
-        fbs[p, pl.ds(2 * c + s, 16, stride=2), :] = v * scale
+        m2[p, pl.ds(BAND + 2 * c + s, 16, stride=2), :] = a2[p, pl.ds(2 * c + s, 16, stride=2), :] - v
 
     soft_rows_copied(l2pr, 2, 0, 128, 2, put_m2)
     exchange(
         "fb", 32, px, pencil,
-        lambda q: fbs.at[:, pl.ds(8 * q, 8)],
+        lambda q: m2.at[:, pl.ds(BAND + 8 * q, 8)],
         lambda q: fbr.at[:, pl.ds(8 * q, 8)],
         fbr.at[:, pl.ds(0, 248)],
     )
@@ -582,51 +586,55 @@
 
     soft_rows(m2, 2, 256, 2, put_w)
     turn2(put_k2)
-    soft_rows(k2, 2, 256, 2, put_w)
     l2s, l2r = ref["l2s"], ref["l2r"]
-
-    def put_l2s(i, j, v):
-        l2s[i, 128 * j : 128 * j + 128, :] = v
-
-    turn2(put_l2s)
 
     low = px < 16
     beside = jnp.where(low, py - 1, py + 1)
     has_beside = (beside >= 0) & (beside < 8)
-    exchange(
-        "l2own", 32, px, pencil,
-        lambda q: l2s.at[:, pl.ds(8 * q, 8)],
-        lambda q: l2r.at[BAND + q],
-        l2r.at[pl.ds(0, 31)],
-    )
-    up, down = ROUNDS.index("l2up"), ROUNDS.index("l2down")
-
-    def to_beside(k, place):
-        def one(q, carry):
-            pltpu.make_async_remote_copy(
-                src_ref=l2s.at[:, pl.ds(8 * q, 8)],
-                dst_ref=l2r.at[place],
-                send_sem=send_sem.at[k],
-                recv_sem=recv_sem.at[k],
-                device_id=(q, beside),
-                device_id_type=MESH,
-            ).start()
-            return carry
-
-        lax.fori_loop(0, 32, one, 0)
-
-    @pl.when(has_beside & low)
-    def _():
-        to_beside(down, 48 + px)
-
-    @pl.when(has_beside & jnp.logical_not(low))
-    def _():
-        to_beside(up, px - 16)
+    k_own = ROUNDS.index("l2own")
+    k_beside = jnp.where(low, ROUNDS.index("l2down"), ROUNDS.index("l2up"))
+    place = jnp.where(low, 48 + px, px - 16)
+
+    def last_send(k, q, row, y):
+        pltpu.make_async_remote_copy(
+            src_ref=l2s.at[:, pl.ds(8 * q, 8)],
+            dst_ref=l2r.at[row],
+            send_sem=send_sem.at[k],
+            recv_sem=recv_sem.at[k],
+            device_id=(q, y),
+            device_id_type=MESH,
+        ).start()
+
+    def last_own():
+        pltpu.make_async_copy(l2s.at[:, pl.ds(8 * px, 8)], l2r.at[BAND + px], recv_sem.at[k_own]).start()
+
+    for i in range(2):
+
+        def put_half(p, c, v, i=i):
+            w3[i, every2(c), :] = v
+
+        soft_rows(k2.at[pl.ds(i, 1)], 1, 256, 2, put_half)
+        for h in range(2):
+            l2s[h, 128 * i : 128 * i + 128, :] = w3[i, 128 * h : 128 * h + 128, :].T
+        to = [16 * i + (px + o) % 16 for o in range(16)]
+
+        def beside_half(to=to):
+            for q in to:
+                last_send(k_beside, q, place, beside)
+
+        pl.when(has_beside)(beside_half)
+        for q in to[1:]:
+            last_send(k_own, q, BAND + px, py)
+        pl.when(px // 16 != i)(functools.partial(last_send, k_own, to[0], BAND + px, py))
+    last_own()
+    leaving.append(("l2own", l2r.at[pl.ds(0, 31)]))
 
     arrived("fb", fbr)
     for d in range(8):
         for h in range(2):
             f_out[d, :, 128 * h : 128 * h + 128] = fbr[h, pl.ds(d, 32, stride=8), :]
+    write_f = pltpu.make_async_copy(f_out, f_into, io_sem.at[2])
+    write_f.start()
 
     arrived("l2own", l2r.at[pl.ds(BAND, 32)])
     edge = jnp.full((BAND, 2, 8, 128), NEG, jnp.float32)
@@ -654,7 +662,9 @@
     for h in range(2):
         cols = slice(128 * h, 128 * h + 128)
         for d in range(8):
-            g_out[d, :, cols] = tgt[d, :, cols] * 0.05 - w3[h, 32 * d : 32 * d + 32, :] * scale
+            g_out[d, :, cols] = w3[h, 32 * d : 32 * d + 32, :]
+    write_g = pltpu.make_async_copy(g_out, g_into, io_sem.at[3])
+    write_g.start()
 
     @pl.when(has_beside & low)
     def _():
@@ -664,6 +674,8 @@
     def _():
         sent("l2up", l2r.at[pl.ds(0, 32)])
 
+    write_f.wait()
+    write_g.wait()
     for name, part in leaving:
         sent(name, part)
     sent("x0", x0r.at[pl.ds(0, 62)])
@@ -673,6 +685,7 @@
 
 
 SCRATCH = [
+    ("src", (8, 32, 256)), ("tgt", (8, 32, 256)), ("f", (8, 32, 256)), ("g", (8, 32, 256)),
     ("g0s", (2, 8, 128)),
     ("g1s", (2, 4, 16, 128)), ("g1r", (8, 2, 2, 16, 128)),
     ("s2ar", (256, 256)),
@@ -685,7 +698,7 @@
     ("l1cs", (2, 128, 128)), ("l1cr", (2, 128, 128)),
     ("l2ps", (2, 128, 128)), ("l2pr", (2, 160, 128)),
     ("l2s", (2, 256, 128)), ("l2r", (64, 2, 8, 128)),
-    ("fbs", (2, 256, 128)), ("fbr", (2, 256, 128)),
+    ("fbr", (2, 256, 128)),
     ("m0", (1, 96, 128)), ("t0", (1, 96, 128)), ("r0", (1, 96, 128)), ("w0", (64, 128)),
     ("a0", (64, 128)), ("b0", (64, 128)),
     ("m1", (2, 160, 128)), ("t1", (2, 160, 128)), ("r1", (2, 160, 128)), ("w1", (2, 128, 128)),
@@ -698,17 +711,18 @@
 
 def per_device(log_source, log_target):
     shape = jax.ShapeDtypeStruct((8, 32, 256), jnp.float32)
-    vmem = pl.BlockSpec(memory_space=pltpu.VMEM)
-    return pl.pallas_call(
+    anywhere = pl.BlockSpec(memory_space=pl.ANY)
+    scaled_f, pulled = pl.pallas_call(
         kernel,
         out_shape=(shape, shape),
-        in_specs=[vmem, vmem],
-        out_specs=(vmem, vmem),
+        in_specs=[anywhere, anywhere],
+        out_specs=(anywhere, anywhere),
         scratch_shapes=[pltpu.VMEM(s, jnp.float32) for _, s in SCRATCH]
-        + [pltpu.SemaphoreType.DMA((len(ROUNDS),)), pltpu.SemaphoreType.DMA((len(ROUNDS),))],
+        + [pltpu.SemaphoreType.DMA((4,)), pltpu.SemaphoreType.DMA((len(ROUNDS),)), pltpu.SemaphoreType.DMA((len(ROUNDS),))],
         compiler_params=pltpu.CompilerParams(collective_id=0, has_side_effects=True),
         name="sinkhorn",
     )(log_source, log_target)
+    return 0.05 * LN2 * scaled_f, 0.05 * log_target - 0.05 * LN2 * pulled
 
 
 def solution(mesh):

time: 87.9 us -> 85.1 us (0.968)
  local copies, waits for them, and re-layouts: 2.42 us -> 0.01 us
  Pallas kernels: 84.7 us -> 82.3 us
  other arithmetic: 0 us -> 1.89 us
    unnamed x4 -> x2, local copies, waits for them, and re-layouts: 2.42 us -> 0.01 us
    pallas_call x1, Pallas kernels: 84.7 us -> 82.3 us  [per_device(): pl.pallas_call(kernel, out_shape=(shape, shape), in_specs=[anywhere, anyw...]
    sub x0 -> x1, other arithmetic: none -> 1.89 us  [per_device(): return (0.05 * LN2 * scaled_f, 0.05 * log_target - 0.05 * LN2 * pulled)]
where the time goes in v5:
time: 85.1 us; the launch traced here: 84.9 us
  Pallas kernels  82.3 us (97%)
  other arithmetic  1.89 us (2%)
    pallas_call x1, Pallas kernels, per_device(): pl.pallas_call(kernel, out_shape=(shape, shape), in_specs=[anywhere, anyw...  82.3 us
    sub x1, other arithmetic, per_device(): return (0.05 * LN2 * scaled_f, 0.05 * log_target - 0.05 * LN2 * pulled)  1.89 us

profile of v5, /device:TPU:1, one launch (start us, length us, event | category | flops | bytes accessed | tf_op | source)
XLA Modules:
  0.0 84.9 jit_solution(9415691791238240493)
XLA Ops:
  0.6 0.0 copy-start
  0.6 82.3 %sinkhorn.1 = (f32[8,32,256]{2,1,0:T(8,128)}, f32[8,32,256]{2,1,0:T(8,128)}) custom-call(f32[8,32,256]{2,1,0:T(8,128)} %src_in.1, f32[8,32,256]{2,1,0:T(8,128)} %tgt_in.1), custom_call_target="tpu_custom_call" | custom-call | tf_op jit(solution)/shard_map/sinkhorn/pallas_call | solution.py:715
  83.0 0.0 copy-done
  83.0 1.9 %multiply_subtract_fusion = (f32[8,32,256]{2,1,0:T(8,128)}, f32[8,32,256]{2,1,0:T(8,128)}) fusion(f32[8,32,256]{2,1,0:T(8,128)} %get-tuple-element.5, f32[8,32,256]{2,1,0:T(8,128)S(1)} %copy-done, f32[8,32,256]{2,1,0:T(8,128)} %get-tuple-element.4), kind=kLoop, calls=%fused_computation | loop fusion | flops 262144 | bytes 1310720 | tf_op jit(solution)/shard_map/sub | solution.py:725
Async XLA Ops:
  0.6 82.4 %copy-start = (f32[8,32,256]{2,1,0:T(8,128)S(1)}, f32[8,32,256]{2,1,0:T(8,128)}, u32[]{:S(2)}) copy-start(f32[8,32,256]{2,1,0:T(8,128)} %tgt_in.1) | copy-start | bytes 786436

commit v6 on v5

--- a/solution.py
+++ b/solution.py
@@ -73,8 +73,9 @@
     return outs
 
 
-def soft_rows(pad, planes, n, level, store, units=4):
+def soft_rows(pad, planes, n, level, store, units=8):
     taps = taps_of(level)
+    units = min(units, n // 16)
     size = 16 * units
     per = n // size
 
@@ -95,7 +96,7 @@
     return pl.ds(start, count, stride=2)
 
 
-def soft_rows_copied(pad, planes, first, n, level, store, chunk=16):
+def soft_rows_copied(pad, planes, first, n, level, store, chunk=32):
     weights = coarse_taps(level)
     per = n // chunk
 
@@ -472,7 +473,7 @@
     c1[0, pl.ds(BAND, 64), :] = mine
 
     def put_u(p, c, s, v):
-        u1[pl.ds(2 * c + s, 16, stride=2), :] = v
+        u1[pl.ds(2 * c + s, 32, stride=2), :] = v
 
     soft_rows_copied(c1, 1, 0, 64, 1, put_u)
     c1[0, pl.ds(BAND, 64), :] = u1[...].T[:64]
@@ -491,7 +492,7 @@
 
     def finish_l1p(b):
         def put(p, c, s, v):
-            m1[b, pl.ds(BAND + 2 * c + s, 16, stride=2), :] = a1[b, pl.ds(2 * c + s, 16, stride=2), :] - v
+            m1[b, pl.ds(BAND + 2 * c + s, 32, stride=2), :] = a1[b, pl.ds(2 * c + s, 32, stride=2), :] - v
 
         return put
 
@@ -539,14 +540,14 @@
     w2, u2, l2ps, l2pr = ref["w2"], ref["u2"], ref["l2ps"], ref["l2pr"]
 
     def put_w2(p, c, s, v):
-        w2[pl.ds(64 * p + 2 * c + s, 16, stride=2), :] = v
+        w2[pl.ds(64 * p + 2 * c + s, 32, stride=2), :] = v
 
     soft_rows_copied(m1, 2, pl.multiple_of(32 * zh, 32), 32, 2, put_w2)
     u2[0, pl.ds(BAND, 128), :] = w2[...].T
     w3 = ref["w3"]
 
     def put_w3(p, c, s, v):
-        w3[0, pl.ds(2 * c + s, 16, stride=2), :] = v
+        w3[0, pl.ds(2 * c + s, 32, stride=2), :] = v
 
     soft_rows_copied(u2, 1, 0, 128, 2, put_w3)
     for h in range(2):
@@ -563,7 +564,7 @@
     m2, k2, fbr = ref["m2"], ref["k2"], ref["fbr"]
 
     def put_m2(p, c, s, v):
-        m2[p, pl.ds(BAND + 2 * c + s, 16, stride=2), :] = a2[p, pl.ds(2 * c + s, 16, stride=2), :] - v
+        m2[p, pl.ds(BAND + 2 * c + s, 32, stride=2), :] = a2[p, pl.ds(2 * c + s, 32, stride=2), :] - v
 
     soft_rows_copied(l2pr, 2, 0, 128, 2, put_m2)
     exchange(
@@ -616,16 +617,17 @@
         soft_rows(k2.at[pl.ds(i, 1)], 1, 256, 2, put_half)
         for h in range(2):
             l2s[h, 128 * i : 128 * i + 128, :] = w3[i, 128 * h : 128 * h + 128, :].T
-        to = [16 * i + (px + o) % 16 for o in range(16)]
+        to = [16 * i + 4 * near[1][dy] + near[0][dx] for dx, dy, dz, dc in FAR_FIRST if dz == dc == 0]
+        to = to + [16 * i + px % 16]
 
         def beside_half(to=to):
             for q in to:
                 last_send(k_beside, q, place, beside)
 
         pl.when(has_beside)(beside_half)
-        for q in to[1:]:
+        for q in to[:-1]:
             last_send(k_own, q, BAND + px, py)
-        pl.when(px // 16 != i)(functools.partial(last_send, k_own, to[0], BAND + px, py))
+        pl.when(px // 16 != i)(functools.partial(last_send, k_own, to[-1], BAND + px, py))
     last_own()
     leaving.append(("l2own", l2r.at[pl.ds(0, 31)]))
 

time: 85.1 us -> 84.6 us (level)
  no operation moved by 1% of the time
where the time goes in v6:
time: 84.6 us; the launch traced here: 84.4 us
  Pallas kernels  81.9 us (97%)
  other arithmetic  1.89 us (2%)
    pallas_call x1, Pallas kernels, per_device(): pl.pallas_call(kernel, out_shape=(shape, shape), in_specs=[anywhere, anyw...  81.9 us
    sub x1, other arithmetic, per_device(): return (0.05 * LN2 * scaled_f, 0.05 * log_target - 0.05 * LN2 * pulled)  1.89 us

profile of v6, /device:TPU:1, one launch (start us, length us, event | category | flops | bytes accessed | tf_op | source)
XLA Modules:
  0.0 84.4 jit_solution(14329304155126068659)
XLA Ops:
  0.6 0.0 copy-start
  0.6 81.9 %sinkhorn.1 = (f32[8,32,256]{2,1,0:T(8,128)}, f32[8,32,256]{2,1,0:T(8,128)}) custom-call(f32[8,32,256]{2,1,0:T(8,128)} %src_in.1, f32[8,32,256]{2,1,0:T(8,128)} %tgt_in.1), custom_call_target="tpu_custom_call" | custom-call | tf_op jit(solution)/shard_map/sinkhorn/pallas_call | solution.py:717
  82.5 0.0 copy-done
  82.6 1.9 %multiply_subtract_fusion = (f32[8,32,256]{2,1,0:T(8,128)}, f32[8,32,256]{2,1,0:T(8,128)}) fusion(f32[8,32,256]{2,1,0:T(8,128)} %get-tuple-element.5, f32[8,32,256]{2,1,0:T(8,128)S(1)} %copy-done, f32[8,32,256]{2,1,0:T(8,128)} %get-tuple-element.4), kind=kLoop, calls=%fused_computation | loop fusion | flops 262144 | bytes 1310720 | tf_op jit(solution)/shard_map/sub | solution.py:727
Async XLA Ops:
  0.6 81.9 %copy-start = (f32[8,32,256]{2,1,0:T(8,128)S(1)}, f32[8,32,256]{2,1,0:T(8,128)}, u32[]{:S(2)}) copy-start(f32[8,32,256]{2,1,0:T(8,128)} %tgt_in.1) | copy-start | bytes 786436

commit v7 on v6

--- a/solution.py
+++ b/solution.py
@@ -249,6 +249,10 @@
             for dx, dy, dz, dc in FAR_FIRST:
                 if dz == 0:
                     to(16 * near[3][dc] + 4 * near[1][dy] + near[0][dx])
+        elif device is pencil:
+            for dx, dy, dz, dc in FAR_FIRST:
+                if dc == 0:
+                    to(16 * near[2][dz] + 4 * near[1][dy] + near[0][dx])
         elif n == 64:
             for dx, dy, dz, dc in FAR_FIRST:
                 to(2 * (16 * near[2][dz] + 4 * near[1][dy] + near[0][dx]) + near[3][dc])

time: 84.6 us -> 83.7 us (0.989)
  no operation moved by 1% of the time
where the time goes in v7:
time: 83.7 us; the launch traced here: 83.6 us
  Pallas kernels  81.1 us (97%)
  other arithmetic  1.89 us (2%)
    pallas_call x1, Pallas kernels, per_device(): pl.pallas_call(kernel, out_shape=(shape, shape), in_specs=[anywhere, anyw...  81.1 us
    sub x1, other arithmetic, per_device(): return (0.05 * LN2 * scaled_f, 0.05 * log_target - 0.05 * LN2 * pulled)  1.89 us

profile of v7, /device:TPU:1, one launch (start us, length us, event | category | flops | bytes accessed | tf_op | source)
XLA Modules:
  0.0 83.6 jit_solution(17053673354192882018)
XLA Ops:
  0.6 0.0 copy-start
  0.6 81.1 %sinkhorn.1 = (f32[8,32,256]{2,1,0:T(8,128)}, f32[8,32,256]{2,1,0:T(8,128)}) custom-call(f32[8,32,256]{2,1,0:T(8,128)} %src_in.1, f32[8,32,256]{2,1,0:T(8,128)} %tgt_in.1), custom_call_target="tpu_custom_call" | custom-call | tf_op jit(solution)/shard_map/sinkhorn/pallas_call | solution.py:721
  81.7 0.0 copy-done
  81.7 1.9 %multiply_subtract_fusion = (f32[8,32,256]{2,1,0:T(8,128)}, f32[8,32,256]{2,1,0:T(8,128)}) fusion(f32[8,32,256]{2,1,0:T(8,128)} %get-tuple-element.5, f32[8,32,256]{2,1,0:T(8,128)S(1)} %copy-done, f32[8,32,256]{2,1,0:T(8,128)} %get-tuple-element.4), kind=kLoop, calls=%fused_computation | loop fusion | flops 262144 | bytes 1310720 | tf_op jit(solution)/shard_map/sub | solution.py:731
Async XLA Ops:
  0.6 81.1 %copy-start = (f32[8,32,256]{2,1,0:T(8,128)S(1)}, f32[8,32,256]{2,1,0:T(8,128)}, u32[]{:S(2)}) copy-start(f32[8,32,256]{2,1,0:T(8,128)} %tgt_in.1) | copy-start | bytes 786436
